TPU v7x, 256 devices: a whole 4x4x8 slice. The times are simulated.
256 devices in a mesh: prop: 8 (over x, core), dom: 32 (over z, y).
Axes of the slice: x: 4, y: 4, z: 8, core: 2. Of those that a mesh axis runs over, the one named last changes fastest.
Arguments:
- states: float32 [8, 128, 64, 128], P('prop', 'dom'), may hold values from -4 to 4
- accepted: int32 [1], replicated, may hold values from 0 to 7
- noise: float32 [8, 128, 64, 128], P('prop', 'dom'), may hold values from -5 to 5
- source: float32 [128, 64, 128], P('dom'), may hold values from -6 to 6
Outputs:
- pressure: float32 [8, 128, 64, 128], P('prop', 'dom')
All inputs are finite; a program needn't handle non-finite values.
Results may differ from a plain program's by a relative error of at most 0.0003.
Values sent between devices are 32-bit elements; how exact they have to be, the bound alone decides.
A program may use at most 128 MiB of HBM per device.

v0:
```python
import math

import jax
import jax.numpy as jnp
from jax import lax
from jax.sharding import PartitionSpec as P

LEVELS = 4
SWEEPS = 2
COARSE_SWEEPS = 64


OMEGA = 0.7
BETA = 0.4
SHRINK = math.sqrt(1.0 - BETA * BETA)
ZSCALE = 16.0


def padded_2(x, sides, width):
    for axis, dim in sides:
        devices, length = (lax.axis_size(axis), x.shape[dim])
        up = [(i, (i + 1) % devices) for i in range(devices - 1)]
        down = [(j, i) for i, j in up]
        last = lax.slice_in_dim(x, length - width, length, axis=dim)
        initial = lax.slice_in_dim(x, 0, width, axis=dim)
        before = lax.ppermute(last, axis, up)
        after = lax.ppermute(initial, axis, down)
        x = jnp.concatenate([before, x, after], axis=dim)
    return x


def from_root(x, axis, root):
    mine = lax.axis_index(axis) == root
    return lax.psum(jnp.where(mine, x, jnp.zeros_like(x)), axis)


def shift_lower(values, axis):
    axis = values.ndim + axis
    count = values.shape[axis]
    kept = lax.slice_in_dim(values, 0, count - 1, axis=axis)
    return jnp.concatenate(
        [jnp.zeros_like(lax.slice_in_dim(values, 0, 1, axis=axis)), kept], axis=axis
    )


def shift_upper(values, axis):
    axis = values.ndim + axis
    count = values.shape[axis]
    kept = lax.slice_in_dim(values, 1, count, axis=axis)
    return jnp.concatenate(
        [kept, jnp.zeros_like(lax.slice_in_dim(values, 0, 1, axis=axis))], axis=axis
    )


def harmonic(first, second):
    return 2.0 * first * second / (first + second)


def coefficients(perm, padded, scale):
    inner_x = harmonic(perm[..., 1:, :], perm[..., :-1, :])
    west = jnp.concatenate([perm[..., :1, :], inner_x], axis=-2)
    east = jnp.concatenate([inner_x, perm[..., -1:, :]], axis=-2)
    inner_y = harmonic(perm[..., 1:], perm[..., :-1])
    south = jnp.concatenate([perm[..., :1], inner_y], axis=-1)
    north = jnp.concatenate([inner_y, perm[..., -1:]], axis=-1)
    below = harmonic(padded[..., :-2, :, :], perm)
    above = harmonic(padded[..., 2:, :, :], perm)
    zfactor = ZSCALE * scale
    parts = [
        west * scale,
        east * scale,
        south * scale,
        north * scale,
        below * zfactor,
        above * zfactor,
    ]
    diagonal = parts[0] + parts[1] + parts[2] + parts[3] + parts[4] + parts[5]
    return parts + [diagonal, OMEGA / diagonal]


def apply_op(values, padded, coefs):
    result = (
        coefs[6] * values - coefs[0] * shift_lower(values, -2) - coefs[1] * shift_upper(values, -2)
    )
    result = result - coefs[2] * shift_lower(values, -1) - coefs[3] * shift_upper(values, -1)
    return result - coefs[4] * padded[..., :-2, :, :] - coefs[5] * padded[..., 2:, :, :]


def sweep(values, right, coefs, pad_z):
    return values + coefs[7] * (right - apply_op(values, pad_z(values), coefs))


def sum_children(values):
    shape = values.shape
    split = values.reshape(shape[:-3] + (shape[-3] // 2, 2, shape[-2] // 2, 2, shape[-1] // 2, 2))
    return split.sum(axis=(-5, -3, -1))


def prolong(values):
    return jnp.repeat(jnp.repeat(jnp.repeat(values, 2, axis=-3), 2, axis=-2), 2, axis=-1)


def zero_pad(values):
    widths = [(0, 0)] * (values.ndim - 3) + [(1, 1), (0, 0), (0, 0)]
    return jnp.pad(values, widths)


def pressure_rim(values):
    return padded_2(values, (("dom", 1),), 1)


def perm_rim(values):
    return padded_2(values, (("dom", 1),), 1)


def coarse_solve(right, perm, level, pad_z, pad_perm):
    coefs = coefficients(perm, pad_perm(perm), 4.0**level)
    start = coefs[7] * right
    return lax.fori_loop(
        0, COARSE_SWEEPS - 1, lambda step, values: sweep(values, right, coefs, pad_z), start
    )


def level_cycle(right, perm, level, pad_z, pad_perm, deeper):
    coefs = coefficients(perm, pad_perm(perm), 4.0**level)
    values = coefs[7] * right
    values = sweep(values, right, coefs, pad_z)
    residue = right - apply_op(values, pad_z(values), coefs)
    update = deeper(sum_children(residue), sum_children(perm) * 0.125, level + 1)
    values = values + prolong(update)
    for step in range(SWEEPS):
        values = sweep(values, right, coefs, pad_z)
    return values


def local_cycle(right, perm, level):
    if level == LEVELS - 1:
        return coarse_solve(right, perm, level, zero_pad, zero_pad)
    return level_cycle(right, perm, level, zero_pad, zero_pad, local_cycle)


def body(states, accepted, noise, source):
    per_device = states.shape[0]
    chosen = accepted[0]
    owner = chosen // per_device
    picked = lax.dynamic_index_in_dim(states, chosen % per_device, 0, keepdims=False)
    current = from_root(picked, "prop", owner)
    theta = SHRINK * current[None] + BETA * noise
    perm = jnp.exp(theta)
    right = source[None]
    gather_level = 2

    def spread_cycle(right_side, field, level):
        if level == gather_level:
            whole_right, whole_perm = (
                lax.all_gather(right_side, "dom", axis=1, tiled=True),
                lax.all_gather(field, "dom", axis=1, tiled=True),
            )
            result = local_cycle(whole_right, whole_perm, level)
            height = right_side.shape[1]
            return lax.dynamic_slice_in_dim(result, lax.axis_index("dom") * height, height, 1)
        return level_cycle(right_side, field, level, pressure_rim, perm_rim, spread_cycle)

    return spread_cycle(right, perm, 0)


def solution(mesh):
    in_specs = (
        P("prop", "dom", None, None),
        P(),
        P("prop", "dom", None, None),
        P("dom", None, None),
    )
    out_specs = P("prop", "dom", None, None)
    return jax.shard_map(body, mesh=mesh, in_specs=in_specs, out_specs=out_specs, check_vma=False)
```

profile of v0, /device:TPU:120, one launch (start us, length us, event | category | flops | bytes accessed | tf_op | source)
XLA Modules:
  0.0 459.8 jit_solution(12875724920466572557)
XLA Ops:
  11.1 65.1 %all-reduce.61.cloned.1.call-done = f32[4,64,128]{1,2,0:T(8,128)} async-done(((f32[4,64,128]{1,2,0:T(8,128)}), f32[4,64,128]{1,2,0:T(8,128)}) %all-reduce.61.cloned.1.call-update) | async-done | bytes 131088 | tf_op jit(solution)/shard_map/psum | solution.py:34
  78.3 9.8 %reshape.767 = f32[2,2,32,2,64,2]{5,4,3,2,1,0:T(8,128)} reshape(f32[1,4,64,128]{3,2,1,0:T(8,128)S(1)} %copy.50) | data formatting | bytes 262144 | tf_op jit(solution)/shard_map/reshape | solution.py:95
  88.1 4.0 reduce_sum.74
  94.8 48.6 %all-gather = f32[512,32]{1,0:T(8,128)S(1)} all-gather(f32[16,32]{1,0:T(8,128)S(1)} %broadcast_multiply_fusion), channel_id=2, replica_groups=mesh['prop'=8,'dom'=32] {'dom'}, dimensions={0}, use_global_device_ids=true | all-gather | bytes 67584 | tf_op jit(solution)/shard_map/all_gather | solution.py:157
  145.8 5.5 %reshape.769 = f32[16,2,8,2,16,2]{3,2,1,0,5,4:T(8,128)} reshape(f32[512,32]{0,1:T(8,128)S(1)} %copy.52) | data formatting | bytes 131072 | tf_op jit(solution)/shard_map/reshape | solution.py:95
  151.4 2.6 reduce_sum.84
  154.2 4.6 collective-permute-start
  160.8 7.2 %collective-permute-start.4 = (f32[1,1,32,64]{3,2,1,0:T(8,128)}, f32[1,1,32,64]{3,2,1,0:T(8,128)S(1)}, u32[]{:S(2)}, u32[]{:S(2)}) collective-permute-start(f32[1,1,32,64]{3,2,1,0:T(8,128)} %get-tuple-element.298), channel_id=1, source_target_pairs={{0,1},{1,2},{2,3},{3,4},{4,5},{5,6},{6,7},{7,8},{8,9},{9,10},{10,1... | collective-permute-start | bytes 24584 | tf_op jit(solution)/shard_map/ppermute | solution.py:26
  179.0 7.2 %collective-permute-start.2 = (f32[1,1,64,128]{2,3,1,0:T(8,128)S(1)}, f32[1,1,64,128]{2,3,1,0:T(8,128)S(1)}, u32[]{:S(2)}, u32[]{:S(2)}) collective-permute-start(f32[1,1,64,128]{2,3,1,0:T(8,128)S(1)} %get-tuple-element.255), channel_id=1, source_target_pairs={{0,1},{1,2},{2,3},{3,4},{4,5},{5,6},{6,7},{7,8},{8,9},{9,10},{10,1... | collective-permute-start | bytes 98312 | tf_op jit(solution)/shard_map/ppermute | solution.py:26
  188.2 7.5 %collective-permute-done.3 = f32[1,1,64,128]{2,3,1,0:T(8,128)S(1)} collective-permute-done((f32[1,1,64,128]{2,3,1,0:T(8,128)S(1)}, f32[1,1,64,128]{2,3,1,0:T(8,128)S(1)}, u32[]{:S(2)}, u32[]{:S(2)}) %collective-permute-start.3) | collective-permute-done | bytes 32800 | tf_op jit(solution)/shard_map/ppermute | solution.py:27
  198.2 3.9 collective-permute-start.7
  202.4 5.2 %collective-permute-done.7 = f32[1,1,64,128]{2,3,1,0:T(8,128)S(1)} collective-permute-done((f32[1,1,64,128]{2,3,1,0:T(8,128)S(1)}, f32[1,1,64,128]{2,3,1,0:T(8,128)S(1)}, u32[]{:S(2)}, u32[]{:S(2)}) %collective-permute-start.7) | collective-permute-done | bytes 32800 | tf_op jit(solution)/shard_map/ppermute | solution.py:27
  208.2 9.8 %reshape.768 = f32[2,2,32,2,64,2]{5,4,3,2,1,0:T(8,128)} reshape(f32[1,4,64,128]{3,2,1,0:T(8,128)S(1)} %copy.51) | data formatting | bytes 262144 | tf_op jit(solution)/shard_map/reshape | solution.py:95
  218.0 4.0 reduce_sum.75
  224.2 3.9 collective-permute-start.9
  228.2 4.9 %collective-permute-done.9 = f32[1,1,32,64]{3,2,1,0:T(8,128)S(1)} collective-permute-done((f32[1,1,32,64]{3,2,1,0:T(8,128)S(1)}, f32[1,1,32,64]{3,2,1,0:T(8,128)S(1)}, u32[]{:S(2)}, u32[]{:S(2)}) %collective-permute-start.9) | collective-permute-done | bytes 8224 | tf_op jit(solution)/shard_map/ppermute | solution.py:27
  233.3 1.9 collective-permute-start.10
  235.2 3.9 collective-permute-start.11
  239.2 4.9 %collective-permute-done.11 = f32[1,1,32,64]{3,2,1,0:T(8,128)S(1)} collective-permute-done((f32[1,1,32,64]{3,2,1,0:T(8,128)S(1)}, f32[1,1,32,64]{3,2,1,0:T(8,128)S(1)}, u32[]{:S(2)}, u32[]{:S(2)}) %collective-permute-start.11) | collective-permute-done | bytes 8224 | tf_op jit(solution)/shard_map/ppermute | solution.py:27
  245.0 46.0 %all-gather.1 = f32[512,32]{1,0:T(8,128)S(1)} all-gather(f32[16,32]{1,0:T(8,128)S(1)} %reduce_sum.82), channel_id=3, replica_groups=mesh['prop'=8,'dom'=32] {'dom'}, dimensions={0}, use_global_device_ids=true | all-gather | bytes 67584 | tf_op jit(solution)/shard_map/all_gather | solution.py:156
  295.8 4.5 reshape.770
  300.3 2.5 reduce_sum.85
  307.9 84.0 %while.15 = (s32[]{:T(128)}, f32[1,16,8,16]{3,2,1,0:T(8,128)S(1)}, f32[1,16,8,16]{3,2,1,0:T(8,128)}, f32[1,16,8,16]{3,2,1,0:T(8,128)}, f32[1,16,8,16]{3,2,1,0:T(...) while((s32[]{:T(128)}, f32[1,16,8,16]{3,2,1,0:T(8,128)S(1)}, ...), condition=%wide.region_10.11_spmd, body=%wide.region_9.10_spmd.sunk | while | flops 32770 | bytes 195701 | solution.py:119
  400.2 4.6 collective-permute-start.12
  406.8 7.0 %collective-permute-done.13 = f32[1,1,32,64]{3,2,1,0:T(8,128)S(1)} collective-permute-done((f32[1,1,32,64]{3,2,1,0:T(8,128)S(1)}, f32[1,1,32,64]{3,2,1,0:T(8,128)S(1)}, u32[]{:S(2)}, u32[]{:S(2)}) %collective-permute-start.13) | collective-permute-done | bytes 8224 | tf_op jit(solution)/shard_map/ppermute | solution.py:27
  416.7 3.9 collective-permute-start.15
  420.7 4.9 %collective-permute-done.15 = f32[1,1,32,64]{3,2,1,0:T(8,128)S(1)} collective-permute-done((f32[1,1,32,64]{3,2,1,0:T(8,128)S(1)}, f32[1,1,32,64]{3,2,1,0:T(8,128)S(1)}, u32[]{:S(2)}, u32[]{:S(2)}) %collective-permute-start.15) | collective-permute-done | bytes 8224 | tf_op jit(solution)/shard_map/ppermute | solution.py:27
  428.8 3.9 collective-permute-start.17
  433.1 5.2 %collective-permute-done.17 = f32[1,1,64,128]{2,3,1,0:T(8,128)S(1)} collective-permute-done((f32[1,1,64,128]{2,3,1,0:T(8,128)S(1)}, f32[1,1,64,128]{2,3,1,0:T(8,128)S(1)}, u32[]{:S(2)}, u32[]{:S(2)}) %collective-permute-start.17) | collective-permute-done | bytes 32800 | tf_op jit(solution)/shard_map/ppermute | solution.py:27
  439.6 1.9 collective-permute-start.18
  441.5 3.9 collective-permute-start.19
  445.8 5.2 %collective-permute-done.19 = f32[1,1,64,128]{2,3,1,0:T(8,128)S(1)} collective-permute-done((f32[1,1,64,128]{2,3,1,0:T(8,128)S(1)}, f32[1,1,64,128]{2,3,1,0:T(8,128)S(1)}, u32[]{:S(2)}, u32[]{:S(2)}) %collective-permute-start.19) | collective-permute-done | bytes 32800 | tf_op jit(solution)/shard_map/ppermute | solution.py:27
  (429 shorter events, 144.2 us)
Async XLA Ops:
  6.5 69.6 %all-reduce.61.cloned.1.call-start = ((), (), s32[]{:S(2)}) async-start(), calls=%async_computation | async-start | bytes 524288 | tf_op jit(solution)/shard_map/psum | solution.py:34
  77.8 129.9 %copy-start.18 = (f32[1,4,64,1]{2,3,1,0:T(1,128)}, f32[1,4,64,1]{2,3,1,0:T(1,128)S(1)}, u32[]{:S(2)}) copy-start(f32[1,4,64,1]{2,3,1,0:T(1,128)S(1)} %get-tuple-element.261) | copy-start | bytes 3076
  77.8 129.9 %copy-start.19 = (f32[1,4,64,1]{2,3,1,0:T(1,128)}, f32[1,4,64,1]{2,3,1,0:T(1,128)S(1)}, u32[]{:S(2)}) copy-start(f32[1,4,64,1]{2,3,1,0:T(1,128)S(1)} %get-tuple-element.262) | copy-start | bytes 3076
  93.3 150.8 %copy-start.8 = (f32[1,2,31,64]{3,2,1,0:T(8,128)}, f32[1,2,31,64]{3,2,1,0:T(8,128)S(1)}, u32[]{:S(2)}) copy-start(f32[1,2,31,64]{3,2,1,0:T(8,128)S(1)} %add_divide_fusion.7) | copy-start | bytes 47620
  154.2 24.2 %collective-permute-start = (f32[1,1,64,128]{2,3,1,0:T(8,128)}, f32[1,1,64,128]{2,3,1,0:T(8,128)S(1)}, u32[]{:S(2)}, u32[]{:S(2)}) collective-permute-start(f32[1,1,64,128]{2,3,1,0:T(8,128)} %get-tuple-element.260), channel_id=1, source_target_pairs={{0,1},{1,2},{2,3},{3,4},{4,5},{5,6},{6,7},{7,8},{8,9},{9,10},{10,1... | collective-permute-start | bytes 98312 | tf_op jit(solution)/shard_map/ppermute | solution.py:26
  158.8 19.6 %collective-permute-start.1 = (f32[1,1,64,128]{2,3,1,0:T(8,128)}, f32[1,1,64,128]{2,3,1,0:T(8,128)S(1)}, u32[]{:S(2)}, u32[]{:S(2)}) collective-permute-start(f32[1,1,64,128]{2,3,1,0:T(8,128)} %get-tuple-element.259), channel_id=1, source_target_pairs={{1,0},{2,1},{3,2},{4,3},{5,4},{6,5},{7,6},{8,7},{9,8},{10,9},{11,1... | collective-permute-start | bytes 98312 | tf_op jit(solution)/shard_map/ppermute | solution.py:27
  160.8 61.3 %collective-permute-start.4 = (f32[1,1,32,64]{3,2,1,0:T(8,128)}, f32[1,1,32,64]{3,2,1,0:T(8,128)S(1)}, u32[]{:S(2)}, u32[]{:S(2)}) collective-permute-start(f32[1,1,32,64]{3,2,1,0:T(8,128)} %get-tuple-element.298), channel_id=1, source_target_pairs={{0,1},{1,2},{2,3},{3,4},{4,5},{5,6},{6,7},{7,8},{8,9},{9,10},{10,1... | collective-permute-start | bytes 24584 | tf_op jit(solution)/shard_map/ppermute | solution.py:26
  168.0 54.1 %collective-permute-start.5 = (f32[1,1,32,64]{3,2,1,0:T(8,128)}, f32[1,1,32,64]{3,2,1,0:T(8,128)S(1)}, u32[]{:S(2)}, u32[]{:S(2)}) collective-permute-start(f32[1,1,32,64]{3,2,1,0:T(8,128)} %get-tuple-element.297), channel_id=1, source_target_pairs={{1,0},{2,1},{3,2},{4,3},{5,4},{6,5},{7,6},{8,7},{9,8},{10,9},{11,1... | collective-permute-start | bytes 24584 | tf_op jit(solution)/shard_map/ppermute | solution.py:27
  170.8 24.9 %copy-start.7 = (f32[1,16,8,16]{2,1,3,0:T(8,128)}, f32[1,16,8,16]{2,1,3,0:T(8,128)S(1)}, u32[]{:S(2)}) copy-start(f32[1,16,8,16]{2,1,3,0:T(8,128)S(1)} %get-tuple-element.188) | copy-start | bytes 24580
  178.5 39.6 %copy-start.1 = (f32[1,1,64,128]{2,3,1,0:T(8,128)}, f32[1,1,64,128]{2,3,1,0:T(8,128)S(1)}, u32[]{:S(2)}) copy-start(f32[1,1,64,128]{2,3,1,0:T(8,128)S(1)} %collective-permute-done) | copy-start | bytes 98308
  178.5 39.6 %copy-start.3 = (f32[1,1,64,128]{2,3,1,0:T(8,128)}, f32[1,1,64,128]{2,3,1,0:T(8,128)S(1)}, u32[]{:S(2)}) copy-start(f32[1,1,64,128]{2,3,1,0:T(8,128)S(1)} %collective-permute-done.1) | copy-start | bytes 98308
  179.0 9.2 %collective-permute-start.2 = (f32[1,1,64,128]{2,3,1,0:T(8,128)S(1)}, f32[1,1,64,128]{2,3,1,0:T(8,128)S(1)}, u32[]{:S(2)}, u32[]{:S(2)}) collective-permute-start(f32[1,1,64,128]{2,3,1,0:T(8,128)S(1)} %get-tuple-element.255), channel_id=1, source_target_pairs={{0,1},{1,2},{2,3},{3,4},{4,5},{5,6},{6,7},{7,8},{8,9},{9,10},{10,1... | collective-permute-start | bytes 98312 | tf_op jit(solution)/shard_map/ppermute | solution.py:26
  186.2 9.5 %collective-permute-start.3 = (f32[1,1,64,128]{2,3,1,0:T(8,128)S(1)}, f32[1,1,64,128]{2,3,1,0:T(8,128)S(1)}, u32[]{:S(2)}, u32[]{:S(2)}) collective-permute-start(f32[1,1,64,128]{2,3,1,0:T(8,128)S(1)} %get-tuple-element.256), channel_id=1, source_target_pairs={{1,0},{2,1},{3,2},{4,3},{5,4},{6,5},{7,6},{8,7},{9,8},{10,9},{11,1... | collective-permute-start | bytes 98312 | tf_op jit(solution)/shard_map/ppermute | solution.py:27
  196.3 6.2 %collective-permute-start.6 = (f32[1,1,64,128]{2,3,1,0:T(8,128)S(1)}, f32[1,1,64,128]{2,3,1,0:T(8,128)S(1)}, u32[]{:S(2)}, u32[]{:S(2)}) collective-permute-start(f32[1,1,64,128]{2,3,1,0:T(8,128)S(1)} %get-tuple-element.249), channel_id=1, source_target_pairs={{0,1},{1,2},{2,3},{3,4},{4,5},{5,6},{6,7},{7,8},{8,9},{9,10},{10,1... | collective-permute-start | bytes 98312 | tf_op jit(solution)/shard_map/ppermute | solution.py:26
  198.2 9.5 %collective-permute-start.7 = (f32[1,1,64,128]{2,3,1,0:T(8,128)S(1)}, f32[1,1,64,128]{2,3,1,0:T(8,128)S(1)}, u32[]{:S(2)}, u32[]{:S(2)}) collective-permute-start(f32[1,1,64,128]{2,3,1,0:T(8,128)S(1)} %get-tuple-element.250), channel_id=1, source_target_pairs={{1,0},{2,1},{3,2},{4,3},{5,4},{6,5},{7,6},{8,7},{9,8},{10,9},{11,1... | collective-permute-start | bytes 98312 | tf_op jit(solution)/shard_map/ppermute | solution.py:27
  222.0 73.8 %copy-start.5 = (f32[2,32,64]{2,1,0:T(8,128)}, f32[2,32,64]{2,1,0:T(8,128)S(1)}, u32[]{:S(2)}) copy-start(f32[2,32,64]{2,1,0:T(8,128)S(1)} %reduce_sum.75) | copy-start | bytes 49156
  222.1 22.1 %copy-start.15 = (f32[1,1,32,64]{3,2,1,0:T(8,128)}, f32[1,1,32,64]{3,2,1,0:T(8,128)S(1)}, u32[]{:S(2)}) copy-start(f32[1,1,32,64]{3,2,1,0:T(8,128)S(1)} %collective-permute-done.4) | copy-start | bytes 24580
  222.1 22.1 %copy-start.16 = (f32[1,1,32,64]{3,2,1,0:T(8,128)}, f32[1,1,32,64]{3,2,1,0:T(8,128)S(1)}, u32[]{:S(2)}) copy-start(f32[1,1,32,64]{3,2,1,0:T(8,128)S(1)} %collective-permute-done.5) | copy-start | bytes 24580
  222.3 5.9 %collective-permute-start.8 = (f32[1,1,32,64]{3,2,1,0:T(8,128)S(1)}, f32[1,1,32,64]{3,2,1,0:T(8,128)S(1)}, u32[]{:S(2)}, u32[]{:S(2)}) collective-permute-start(f32[1,1,32,64]{3,2,1,0:T(8,128)S(1)} %get-tuple-element.293), channel_id=1, source_target_pairs={{0,1},{1,2},{2,3},{3,4},{4,5},{5,6},{6,7},{7,8},{8,9},{9,10},{10,1... | collective-permute-start | bytes 24584 | tf_op jit(solution)/shard_map/ppermute | solution.py:26
  224.2 9.0 %collective-permute-start.9 = (f32[1,1,32,64]{3,2,1,0:T(8,128)S(1)}, f32[1,1,32,64]{3,2,1,0:T(8,128)S(1)}, u32[]{:S(2)}, u32[]{:S(2)}) collective-permute-start(f32[1,1,32,64]{3,2,1,0:T(8,128)S(1)} %get-tuple-element.294), channel_id=1, source_target_pairs={{1,0},{2,1},{3,2},{4,3},{5,4},{6,5},{7,6},{8,7},{9,8},{10,9},{11,1... | collective-permute-start | bytes 24584 | tf_op jit(solution)/shard_map/ppermute | solution.py:27
  233.3 5.9 %collective-permute-start.10 = (f32[1,1,32,64]{3,2,1,0:T(8,128)S(1)}, f32[1,1,32,64]{3,2,1,0:T(8,128)S(1)}, u32[]{:S(2)}, u32[]{:S(2)}) collective-permute-start(f32[1,1,32,64]{3,2,1,0:T(8,128)S(1)} %get-tuple-element.287), channel_id=1, source_target_pairs={{0,1},{1,2},{2,3},{3,4},{4,5},{5,6},{6,7},{7,8},{8,9},{9,10},{10,1... | collective-permute-start | bytes 24584 | tf_op jit(solution)/shard_map/ppermute | solution.py:26
  235.2 9.0 %collective-permute-start.11 = (f32[1,1,32,64]{3,2,1,0:T(8,128)S(1)}, f32[1,1,32,64]{3,2,1,0:T(8,128)S(1)}, u32[]{:S(2)}, u32[]{:S(2)}) collective-permute-start(f32[1,1,32,64]{3,2,1,0:T(8,128)S(1)} %get-tuple-element.288), channel_id=1, source_target_pairs={{1,0},{2,1},{3,2},{4,3},{5,4},{6,5},{7,6},{8,7},{9,8},{10,9},{11,1... | collective-permute-start | bytes 24584 | tf_op jit(solution)/shard_map/ppermute | solution.py:27
  397.3 41.0 %copy-start.2 = (f32[1,1,64,128]{2,3,1,0:T(8,128)S(1)}, f32[1,1,64,128]{2,3,1,0:T(8,128)}, u32[]{:S(2)}) copy-start(f32[1,1,64,128]{2,3,1,0:T(8,128)} %copy-done.1) | copy-start | bytes 98308
  397.3 41.0 %copy-start.4 = (f32[1,1,64,128]{2,3,1,0:T(8,128)S(1)}, f32[1,1,64,128]{2,3,1,0:T(8,128)}, u32[]{:S(2)}) copy-start(f32[1,1,64,128]{2,3,1,0:T(8,128)} %copy-done.3) | copy-start | bytes 98308
  400.2 6.6 %collective-permute-start.12 = (f32[1,1,32,64]{3,2,1,0:T(8,128)S(1)}, f32[1,1,32,64]{3,2,1,0:T(8,128)S(1)}, u32[]{:S(2)}, u32[]{:S(2)}) collective-permute-start(f32[1,1,32,64]{3,2,1,0:T(8,128)S(1)} %get-tuple-element.279), channel_id=1, source_target_pairs={{0,1},{1,2},{2,3},{3,4},{4,5},{5,6},{6,7},{7,8},{8,9},{9,10},{10,1... | collective-permute-start | bytes 24584 | tf_op jit(solution)/shard_map/ppermute | solution.py:26
  404.8 9.0 %collective-permute-start.13 = (f32[1,1,32,64]{3,2,1,0:T(8,128)S(1)}, f32[1,1,32,64]{3,2,1,0:T(8,128)S(1)}, u32[]{:S(2)}, u32[]{:S(2)}) collective-permute-start(f32[1,1,32,64]{3,2,1,0:T(8,128)S(1)} %get-tuple-element.280), channel_id=1, source_target_pairs={{1,0},{2,1},{3,2},{4,3},{5,4},{6,5},{7,6},{8,7},{9,8},{10,9},{11,1... | collective-permute-start | bytes 24584 | tf_op jit(solution)/shard_map/ppermute | solution.py:27
  414.7 5.9 %collective-permute-start.14 = (f32[1,1,32,64]{3,2,1,0:T(8,128)S(1)}, f32[1,1,32,64]{3,2,1,0:T(8,128)S(1)}, u32[]{:S(2)}, u32[]{:S(2)}) collective-permute-start(f32[1,1,32,64]{3,2,1,0:T(8,128)S(1)} %get-tuple-element.273), channel_id=1, source_target_pairs={{0,1},{1,2},{2,3},{3,4},{4,5},{5,6},{6,7},{7,8},{8,9},{9,10},{10,1... | collective-permute-start | bytes 24584 | tf_op jit(solution)/shard_map/ppermute | solution.py:26
  416.7 9.0 %collective-permute-start.15 = (f32[1,1,32,64]{3,2,1,0:T(8,128)S(1)}, f32[1,1,32,64]{3,2,1,0:T(8,128)S(1)}, u32[]{:S(2)}, u32[]{:S(2)}) collective-permute-start(f32[1,1,32,64]{3,2,1,0:T(8,128)S(1)} %get-tuple-element.274), channel_id=1, source_target_pairs={{1,0},{2,1},{3,2},{4,3},{5,4},{6,5},{7,6},{8,7},{9,8},{10,9},{11,1... | collective-permute-start | bytes 24584 | tf_op jit(solution)/shard_map/ppermute | solution.py:27
  426.9 6.2 %collective-permute-start.16 = (f32[1,1,64,128]{2,3,1,0:T(8,128)S(1)}, f32[1,1,64,128]{2,3,1,0:T(8,128)S(1)}, u32[]{:S(2)}, u32[]{:S(2)}) collective-permute-start(f32[1,1,64,128]{2,3,1,0:T(8,128)S(1)} %get-tuple-element.219), channel_id=1, source_target_pairs={{0,1},{1,2},{2,3},{3,4},{4,5},{5,6},{6,7},{7,8},{8,9},{9,10},{10,1... | collective-permute-start | bytes 98312 | tf_op jit(solution)/shard_map/ppermute | solution.py:26
  428.8 9.5 %collective-permute-start.17 = (f32[1,1,64,128]{2,3,1,0:T(8,128)S(1)}, f32[1,1,64,128]{2,3,1,0:T(8,128)S(1)}, u32[]{:S(2)}, u32[]{:S(2)}) collective-permute-start(f32[1,1,64,128]{2,3,1,0:T(8,128)S(1)} %get-tuple-element.220), channel_id=1, source_target_pairs={{1,0},{2,1},{3,2},{4,3},{5,4},{6,5},{7,6},{8,7},{9,8},{10,9},{11,1... | collective-permute-start | bytes 98312 | tf_op jit(solution)/shard_map/ppermute | solution.py:27
  439.6 6.2 %collective-permute-start.18 = (f32[1,1,64,128]{2,3,1,0:T(8,128)S(1)}, f32[1,1,64,128]{2,3,1,0:T(8,128)S(1)}, u32[]{:S(2)}, u32[]{:S(2)}) collective-permute-start(f32[1,1,64,128]{2,3,1,0:T(8,128)S(1)} %get-tuple-element.213), channel_id=1, source_target_pairs={{0,1},{1,2},{2,3},{3,4},{4,5},{5,6},{6,7},{7,8},{8,9},{9,10},{10,1... | collective-permute-start | bytes 98312 | tf_op jit(solution)/shard_map/ppermute | solution.py:26
  441.5 9.5 %collective-permute-start.19 = (f32[1,1,64,128]{2,3,1,0:T(8,128)S(1)}, f32[1,1,64,128]{2,3,1,0:T(8,128)S(1)}, u32[]{:S(2)}, u32[]{:S(2)}) collective-permute-start(f32[1,1,64,128]{2,3,1,0:T(8,128)S(1)} %get-tuple-element.214), channel_id=1, source_target_pairs={{1,0},{2,1},{3,2},{4,3},{5,4},{6,5},{7,6},{8,7},{9,8},{10,9},{11,1... | collective-permute-start | bytes 98312 | tf_op jit(solution)/shard_map/ppermute | solution.py:27
  (11 other events, 156.1 us)
Sparse Core Ops, SparseCore 0:
  9.7 66.4 all-reduce.60
where the time goes:
time: 465 us; the launch traced here: 460 us
  waiting for transfers between devices  111 us (24%)
  other arithmetic  108 us (23%)
  blocking collectives  94.6 us (20%)
  starting transfers between devices  66.4 us (14%)
  local copies, waits for them, and re-layouts  62.8 us (14%)
  between operations  15 us (3%)
    add x71, other arithmetic, sweep(): return values + coefs[7] * (right - apply_op(values, pad_z(values), coefs))  82.6 us
    psum x1, waiting for transfers between devices, from_root(): return lax.psum(jnp.where(mine, x, jnp.zeros_like(x)), axis)  65.1 us
    all_gather x1, blocking collectives, spread_cycle(): lax.all_gather(field, 'dom', axis=1, tiled=True)  48.6 us
    all_gather x1, blocking collectives, spread_cycle(): lax.all_gather(right_side, 'dom', axis=1, tiled=True)  46 us
    ppermute x10, waiting for transfers between devices, padded_2(): after = lax.ppermute(initial, axis, down)  45.1 us
    ppermute x10, starting transfers between devices, padded_2(): before = lax.ppermute(last, axis, up)  35.2 us
    ppermute x10, starting transfers between devices, padded_2(): after = lax.ppermute(initial, axis, down)  31.2 us
    reshape x4, local copies, waits for them, and re-layouts, sum_children(): values.reshape(shape[:-3] + (shape[-3] // 2, 2, shape[-2] // 2, 2, shape[...  29.6 us
  transfers between devices with their start and end apart: 21, of which 12 were waited for; matrix products, arithmetic and copies ran while one was open for 6% of the time, Pallas kernels for 0%

commit v1 on v0

v1 whole, which is shorter than its diff:
```python
import functools
import math

import jax
import jax.numpy as jnp
from jax import lax
from jax.experimental import pallas as pl
from jax.experimental.pallas import tpu as pltpu
from jax.sharding import PartitionSpec as P

OMEGA = 0.7
BETA = 0.4
SHRINK = math.sqrt(1.0 - BETA * BETA)
KEEP = 1.0 - OMEGA
COARSE_SWEEPS = 64
F32 = jnp.float32
BF16 = jnp.bfloat16
MESH = pl.DeviceIdType.MESH


def iota(shape, axis):
    return lax.broadcasted_iota(jnp.int32, shape, axis)


def ones_where(mask):
    return jnp.where(mask, 1.0, 0.0).astype(BF16)


def dot3(x, matrix):
    rows = x.shape[0]
    hi = x.astype(BF16).astype(F32)
    rest = x - hi
    mid = rest.astype(BF16).astype(F32)
    stacked = jnp.concatenate([hi, mid, rest - mid], axis=0).astype(BF16)
    y = jnp.dot(stacked, matrix, preferred_element_type=F32)
    return y[:rows] + y[rows : 2 * rows] + y[2 * rows :]


def up(v, axis, by=1):
    return pltpu.roll(v, v.shape[axis] - by, axis)


def down(v, axis, by=1):
    return pltpu.roll(v, by, axis)


def harmonic(a, b):
    return 2.0 * a * b / (a + b)


def pair_rows(ref, rows):
    return ref[pl.ds(0, rows, stride=2), :] + ref[pl.ds(1, rows, stride=2), :]


def repeat_rows(ref, value):
    rows = value.shape[0]
    ref[pl.ds(0, rows, stride=2), :] = value
    ref[pl.ds(1, rows, stride=2), :] = value


def zup1(v):
    swapped = pltpu.roll(v, 64, 1)
    return jnp.where(iota(v.shape, 1) < 64, swapped, up(swapped, 0, 32))


def zdown1(v):
    swapped = pltpu.roll(v, 64, 1)
    return jnp.where(iota(v.shape, 1) < 64, down(swapped, 0, 32), swapped)


def zup2(v):
    moved = up(v, 1, 32)
    return jnp.where(iota(v.shape, 1) < 96, moved, up(moved, 0, 16))


def zdown2(v):
    moved = down(v, 1, 32)
    return jnp.where(iota(v.shape, 1) < 32, down(moved, 0, 16), moved)


def flat_coefs(perm, scale, nx, ny, zup, zdown, top):
    x = lax.rem(iota(perm.shape, 0), nx)
    y = lax.rem(iota(perm.shape, 1), ny)
    east = jnp.where(x < nx - 1, scale * harmonic(perm, up(perm, 0)), 0.0)
    north = jnp.where(y < ny - 1, scale * harmonic(perm, up(perm, 1)), 0.0)
    above = jnp.where(top, 0.0, (16.0 * scale) * harmonic(perm, zup(perm)))
    west, south, below = down(east, 0), down(north, 1), zdown(above)
    edges = jnp.where(x == 0, scale, 0.0) + jnp.where(x == nx - 1, scale, 0.0)
    edges = edges + jnp.where(y == 0, scale, 0.0) + jnp.where(y == ny - 1, scale, 0.0)
    diag = west + east + south + north + below + above + edges * perm
    return west, east, south, north, below, above, diag, OMEGA / diag


def around(v, c, zup, zdown):
    a = c[0] * down(v, 0) + c[1] * up(v, 0)
    b = c[2] * down(v, 1) + c[3] * up(v, 1)
    return (a + b) + (c[4] * zdown(v) + c[5] * zup(v))


def kernel(
    props, doms, acc_ref, states, noise, source, out_ref,
    rx, cur, nz, perm, src, cw, ce, cs, cn, cu, dg, cc, va, vb, tmp,
    perm1, right1, tmp1, co1, v1s, tmp2, gp2, gr2, tmp3, e2s,
    loc, s1, d1, s2, d2, ss, ds_, sn, dn, sf, df, sq, dq, sp, dp, sr, dr, sg, dgs,
):
    me = lax.axis_index("prop")
    dom = lax.axis_index("dom")

    def peer(o):
        return lax.rem(me + o, props)

    def slab(o):
        return lax.rem(dom + (o + doms), doms)

    def remote(from_ref, to_ref, send, recv, p, d):
        return pltpu.make_async_remote_copy(
            src_ref=from_ref, dst_ref=to_ref, send_sem=send, recv_sem=recv,
            device_id=(p, d), device_id_type=MESH,
        )

    load_noise = pltpu.make_async_copy(noise, nz, loc.at[0])
    load_source = pltpu.make_async_copy(source, src.at[pl.ds(4, 4)], loc.at[1])
    load_piece = pltpu.make_async_copy(states.at[me], rx.at[me], loc.at[2])
    load_piece.start()
    load_noise.start()
    load_source.start()

    barrier = pltpu.get_barrier_semaphore()
    for o in range(1, props):
        pl.semaphore_signal(barrier, inc=1, device_id=(peer(o), dom), device_id_type=MESH)

    def greet(o, carry):
        pl.semaphore_signal(barrier, inc=1, device_id=(me, slab(o)), device_id_type=MESH)
        return carry

    lax.fori_loop(1, doms, greet, 0)
    pl.semaphore_wait(barrier, props + doms - 2)

    sends1 = []
    for o in range(1, props):
        copy = remote(states.at[peer(o)], rx.at[me], s1.at[o - 1], d1.at[o - 1], peer(o), dom)
        copy.start()
        sends1.append(copy)
    sends_src = [
        remote(source, src.at[pl.ds(0, 4)], ss.at[0], ds_.at[0], me, slab(1)),
        remote(source, src.at[pl.ds(8, 4)], ss.at[1], ds_.at[1], me, slab(-1)),
    ]
    for copy in sends_src:
        copy.start()

    r01, l01 = iota((256, 128), 0), iota((256, 128), 1)
    c01 = ones_where(l01 == (r01 // 128) * 64 + lax.rem(r01, 128) // 2)
    r12, l12 = iota((128, 32), 0), iota((128, 32), 1)
    c12 = ones_where(l12 == lax.rem(r12, 64) // 2)
    r23, l23 = iota((128, 256), 0), iota((128, 256), 1)
    c23 = ones_where((r23 // 64 == l23 // 128) & (lax.rem(r23, 32) // 2 == lax.rem(l23, 16)))
    r32, l32 = iota((256, 128), 0), iota((256, 128), 1)
    c32 = ones_where((l32 // 64 == r32 // 128) & (lax.rem(l32, 32) // 2 == lax.rem(r32, 16)))
    r21, l21 = iota((128, 128), 0), iota((128, 128), 1)
    c21 = ones_where(lax.rem(l21, 64) // 2 == lax.rem(r21, 32))
    r10, l10 = iota((128, 256), 0), iota((128, 256), 1)
    c10 = ones_where((r10 // 64 == l10 // 128) & (lax.rem(r10, 64) == lax.rem(l10, 128) // 2))
    row, lane = iota((64, 128), 0), iota((64, 128), 1)
    east_in, north_in = row < 63, lane < 127
    edges = jnp.where(row == 0, 1.0, 0.0) + jnp.where(row == 63, 1.0, 0.0)
    edges = edges + jnp.where(lane == 0, 1.0, 0.0) + jnp.where(lane == 127, 1.0, 0.0)

    load_piece.wait()
    for copy in sends1:
        copy.wait_recv()
    cur[me] = rx[acc_ref[0]]
    sends2 = []
    for o in range(1, props):
        copy = remote(cur.at[me], cur.at[me], s2.at[o - 1], d2.at[o - 1], peer(o), dom)
        copy.start()
        sends2.append(copy)
    load_noise.wait()
    for copy in sends2:
        copy.wait_recv()

    theta = SHRINK * cur[...] + BETA * nz[...]
    perm[pl.ds(4, 4)] = jnp.exp(theta).reshape(4, 64, 128)

    near = [
        remote(perm.at[pl.ds(5, 3)], perm.at[pl.ds(1, 3)], sn.at[0], dn.at[0], me, slab(1)),
        remote(perm.at[pl.ds(4, 3)], perm.at[pl.ds(8, 3)], sn.at[1], dn.at[1], me, slab(-1)),
    ]
    far = [
        remote(perm.at[4], perm.at[0], sf.at[0], df.at[0], me, slab(1)),
        remote(perm.at[7], perm.at[11], sf.at[1], df.at[1], me, slab(-1)),
    ]
    for copy in near:
        copy.start()

    def restrict01(planes):
        sums = []
        for i in range(2):
            tmp[...] = planes[2 * i] + planes[2 * i + 1]
            sums.append(pair_rows(tmp, 32))
        return dot3(jnp.concatenate(sums, axis=1), c01)

    def restrict12(value):
        tmp2[pl.ds(0, 32)] = value
        return dot3(pair_rows(tmp2, 16), c12)

    own1 = 0.125 * restrict01([perm[k] for k in range(4, 8)])
    perm1[3] = own1
    sends_q = []
    for i, o in enumerate((1, -1, 2, -2, 3, -3)):
        copy = remote(perm1.at[3], perm1.at[3 - o], sq.at[i], dq.at[i], me, slab(o))
        copy.start()
        sends_q.append(copy)
    for copy in far:
        copy.start()
    gp2[dom] = 0.125 * restrict12(own1)

    def gather_to(buf, send, recv):
        def go(o, carry):
            remote(buf.at[dom], buf.at[dom], send, recv, me, slab(o)).start()
            return carry

        lax.fori_loop(1, doms, go, 0)

    def gather_wait(buf, send, recv):
        part = buf.at[pl.ds(0, doms - 1)]
        return remote(part, part, send, recv, me, slab(1))

    gather_to(gp2, sp.at[0], dp.at[0])

    def sides(k):
        p = perm[k]
        east = jnp.where(east_in, harmonic(p, up(p, 0)), 0.0)
        north = jnp.where(north_in, harmonic(p, up(p, 1)), 0.0)
        ce[k] = east
        cn[k] = north
        cw[k] = down(east, 0)
        cs[k] = down(north, 1)

    inside_low = jnp.where(dom == 0, 0.0, 16.0)
    inside_high = jnp.where(dom == doms - 1, 0.0, 16.0)

    def face(k):
        factor = {3: inside_low, 7: inside_high}.get(k, 16.0)
        cu[k] = factor * harmonic(perm[k], perm[k + 1])

    def finish(k):
        diag = cw[k] + ce[k] + cs[k] + cn[k] + cu[k - 1] + cu[k] + edges * perm[k]
        dg[k] = diag
        scaled = OMEGA / diag
        cc[k] = scaled
        va[k] = scaled * src[k]

    def around0(v, k):
        x = v[k]
        a = cw[k] * down(x, 0) + ce[k] * up(x, 0)
        b = cs[k] * down(x, 1) + cn[k] * up(x, 1)
        return x, (a + b) + (cu[k - 1] * v[k - 1] + cu[k] * v[k + 1])

    def sweep0(v, k):
        x, total = around0(v, k)
        return KEEP * x + cc[k] * (src[k] + total)

    for k in range(4, 8):
        sides(k)
    for k in range(4, 7):
        face(k)
    load_source.wait()
    for copy in sends_src:
        copy.wait_recv()
    finish(5)
    finish(6)
    for copy in near:
        copy.wait_recv()
    for k in (2, 3, 8, 9):
        sides(k)
    for k in (1, 2, 3, 7, 8, 9):
        face(k)
    for k in (2, 3, 4, 7, 8, 9):
        finish(k)
    for k in range(3, 9):
        vb[k] = sweep0(va, k)
    rest = []
    for k in range(4, 8):
        x, total = around0(vb, k)
        rest.append(src[k] - dg[k] * x + total)
    right1[2] = restrict01(rest)
    sends_r = []
    for i, o in enumerate((1, -1, 2, -2)):
        copy = remote(right1.at[2], right1.at[2 - o], sr.at[i], dr.at[i], me, slab(o))
        copy.start()
        sends_r.append(copy)

    for copy in sends_q:
        copy.wait_recv()
    wide = perm1[...].reshape(7 * 32, 128)
    pair = lax.rem(dom + (doms - 3) + iota(wide.shape, 0) // 32, doms)
    top1 = (pair == doms - 1) & (iota(wide.shape, 1) >= 64)
    for i, value in enumerate(flat_coefs(wide, 4.0, 32, 64, zup1, zdown1, top1)):
        co1[i] = value[32:192]
    for copy in far:
        copy.wait_recv()
    for k in (1, 10):
        sides(k)
    for k in (0, 10):
        face(k)
    for k in (1, 10):
        finish(k)
    for k in (2, 9):
        vb[k] = sweep0(va, k)

    for copy in sends_r:
        copy.wait_recv()
    b1 = right1[...].reshape(160, 128)
    first = co1[7] * b1
    v1 = KEEP * first + co1[7] * (b1 + around(first, co1, zup1, zdown1))
    v1s[...] = v1
    res1 = b1 - co1[6] * v1 + around(v1, co1, zup1, zdown1)
    gr2[dom] = restrict12(res1[64:96])
    gather_to(gr2, sg.at[0], dgs.at[0])

    def whole(buf):
        groups = []
        for g in range(doms // 4):
            groups.append(jnp.concatenate([buf[4 * g + i] for i in range(4)], axis=1))
        return jnp.concatenate(groups, axis=0)

    rows3, lanes3 = iota((64, 256), 0), iota((64, 256), 1)
    mask3 = rows3 // 8 == lax.rem(lanes3, 128) // 16

    def restrict23(value):
        tmp3[...] = value
        y = jnp.where(mask3, dot3(pair_rows(tmp3, 64), c23), 0.0)
        total = y[0:8]
        for g in range(1, 8):
            total = total + y[8 * g : 8 * g + 8]
        return total[:, :128], total[:, 128:]

    gather_wait(gp2, sp.at[0], dp.at[0]).wait_recv()
    p2 = whole(gp2)
    top2 = (iota(p2.shape, 0) >= 112) & (iota(p2.shape, 1) >= 96)
    co2 = flat_coefs(p2, 16.0, 16, 32, zup2, zdown2, top2)
    pa, pb = restrict23(p2)
    pa, pb = 0.125 * pa, 0.125 * pb
    x3, lane3 = iota((8, 128), 0), iota((8, 128), 1)
    y3 = lax.rem(lane3, 16)
    scale = 64.0
    edges3 = jnp.where(x3 == 0, scale, 0.0) + jnp.where(x3 == 7, scale, 0.0)
    edges3 = edges3 + jnp.where(y3 == 0, scale, 0.0) + jnp.where(y3 == 15, scale, 0.0)

    def sides3(p):
        east = jnp.where(x3 < 7, scale * harmonic(p, up(p, 0)), 0.0)
        north = jnp.where(y3 < 15, scale * harmonic(p, up(p, 1)), 0.0)
        return [down(east, 0), east, down(north, 1), north]

    mid = (16.0 * scale) * harmonic(pa, pb)
    high = jnp.where(lane3 < 112, (16.0 * scale) * harmonic(pb, up(pa, 1, 16)), 0.0)
    low = down(high, 1, 16)
    ca = sides3(pa) + [low, mid]
    cb = sides3(pb) + [mid, high]

    def scaled3(c, p):
        inverse = OMEGA / ((c[0] + c[1]) + (c[2] + c[3]) + (c[4] + c[5]) + edges3 * p)
        return inverse, [inverse * value for value in c]

    ia, ca = scaled3(ca, pa)
    ib, cb = scaled3(cb, pb)

    gather_wait(gr2, sg.at[0], dgs.at[0]).wait_recv()
    b2 = whole(gr2)
    first = co2[7] * b2
    v2 = KEEP * first + co2[7] * (b2 + around(first, co2, zup2, zdown2))
    res2 = b2 - co2[6] * v2 + around(v2, co2, zup2, zdown2)
    ra, rb = restrict23(res2)
    ga, gb = ia * ra, ib * rb

    def near3(v, c, base):
        a = c[0] * down(v, 0) + c[1] * up(v, 0)
        b = c[2] * down(v, 1) + c[3] * up(v, 1)
        return (a + b) + (KEEP * v + base)

    def coarse(step, pair_):
        a, b = pair_
        new_a = near3(a, ca, ga) + (ca[4] * down(b, 1, 16) + ca[5] * b)
        new_b = near3(b, cb, gb) + (cb[4] * a + cb[5] * up(a, 1, 16))
        return new_a, new_b

    ea, eb = lax.fori_loop(0, COARSE_SWEEPS - 1, coarse, (ga, gb))
    e3 = jnp.concatenate([jnp.concatenate([ea, eb], axis=1)] * 8, axis=0)
    repeat_rows(tmp3, dot3(jnp.where(mask3, e3, 0.0), c32))
    v2 = v2 + tmp3[...]
    for _ in range(2):
        v2 = KEEP * v2 + co2[7] * (b2 + around(v2, co2, zup2, zdown2))
    e2s[...] = v2

    parts = []
    lane2 = iota((16, 128), 1) // 32
    for j in range(-2, 3):
        z = slab(j)
        value = e2s[pl.ds(pl.multiple_of((z // 4) * 16, 16), 16), :]
        parts.append(jnp.where(lane2 == lax.rem(z, 4), value, 0.0))
    repeat_rows(tmp1, dot3(jnp.concatenate(parts, axis=0), c21))
    v1 = v1s[...] + tmp1[...]
    b1 = right1[...].reshape(160, 128)
    for _ in range(2):
        v1 = KEEP * v1 + co1[7] * (b1 + around(v1, co1, zup1, zdown1))

    fine = dot3(v1[32:128], c10)
    for k, i, half in ((2, 0, 1), (4, 1, 0), (6, 1, 1), (8, 2, 0)):
        repeat_rows(tmp, fine[32 * i : 32 * i + 32, 128 * half : 128 * half + 128])
        add = tmp[...]
        vb[k] = vb[k] + add
        vb[k + 1] = vb[k + 1] + add
    for k in range(3, 9):
        va[k] = sweep0(vb, k)
    for k in range(4, 8):
        out_ref[k - 4] = sweep0(va, k)

    for copies in (sends1, sends2, sends_src, near, far, sends_q, sends_r):
        for copy in copies:
            copy.wait_send()
    gather_wait(gp2, sp.at[0], dp.at[0]).wait_send()
    gather_wait(gr2, sg.at[0], dgs.at[0]).wait_send()


def body(states, accepted, noise, source):
    props, doms = lax.axis_size("prop"), lax.axis_size("dom")
    rows = 256 // props
    dma = pltpu.SemaphoreType.DMA
    plane = lambda n: pltpu.VMEM((n, 64, 128), F32)
    scratch = [
        pltpu.VMEM((props, rows, 128), F32),
        pltpu.VMEM((props, rows, 128), F32),
        pltpu.VMEM((props, rows, 128), F32),
        plane(12), plane(12),
        plane(12), plane(12), plane(12), plane(12), plane(12), plane(12), plane(12),
        plane(12), plane(12),
        pltpu.VMEM((64, 128), F32),
        pltpu.VMEM((7, 32, 128), F32),
        pltpu.VMEM((5, 32, 128), F32),
        pltpu.VMEM((160, 128), F32),
        pltpu.VMEM((8, 160, 128), F32),
        pltpu.VMEM((160, 128), F32),
        pltpu.VMEM((32, 128), F32),
        pltpu.VMEM((doms, 16, 32), F32),
        pltpu.VMEM((doms, 16, 32), F32),
        pltpu.VMEM((128, 128), F32),
        pltpu.VMEM((128, 128), F32),
        dma((3,)),
        dma((props - 1,)), dma((props - 1,)), dma((props - 1,)), dma((props - 1,)),
        dma((2,)), dma((2,)), dma((2,)), dma((2,)), dma((2,)), dma((2,)),
        dma((6,)), dma((6,)), dma((1,)), dma((1,)), dma((4,)), dma((4,)), dma((1,)), dma((1,)),
    ]
    hbm = pl.BlockSpec(memory_space=pl.ANY)
    out = pl.pallas_call(
        functools.partial(kernel, props, doms),
        out_shape=jax.ShapeDtypeStruct((4, 64, 128), F32),
        in_specs=[pl.BlockSpec(memory_space=pltpu.SMEM), hbm, hbm, hbm],
        out_specs=pl.BlockSpec(memory_space=pltpu.VMEM),
        scratch_shapes=scratch,
        compiler_params=pltpu.CompilerParams(collective_id=0, has_side_effects=True),
        name="mcmc_step",
    )(
        accepted,
        states.reshape(props, rows, 128),
        noise.reshape(props, rows, 128),
        source,
    )
    return out[None]


def solution(mesh):
    in_specs = (
        P("prop", "dom", None, None),
        P(),
        P("prop", "dom", None, None),
        P("dom", None, None),
    )
    out_specs = P("prop", "dom", None, None)
    return jax.shard_map(body, mesh=mesh, in_specs=in_specs, out_specs=out_specs, check_vma=False)
```

time: 465 us -> 50.9 us (0.11)
  the two profiles are of different devices: /device:TPU:120 before, /device:TPU:1 now
where the time goes in v1:
time: 50.9 us; the launch traced here: 50.8 us
  Pallas kernels  48.5 us (95%)
  local copies, waits for them, and re-layouts  1.57 us (3%)
  between operations  0.66 us (1%)
    pallas_call x1, Pallas kernels, body(): pl.pallas_call(functools.partial(kernel, props, doms), out_shape=jax.Shap...  48.5 us
    unnamed x1, local copies, waits for them, and re-layouts  1.57 us

profile of v1, /device:TPU:1, one launch (start us, length us, event | category | flops | bytes accessed | tf_op | source)
XLA Modules:
  0.0 50.8 jit_solution(4926348703827941984)
XLA Ops:
  0.7 48.5 %mcmc_step.1 = f32[4,64,128]{2,1,0:T(8,128)} custom-call(s32[1]{0:T(128)S(6)} %copy.6.acc_ref, f32[8,32,128]{2,1,0:T(8,128)} %bitcast.4, f32[8,32,128]{2,1,0:T(8,128)} %bitcast.5, f32[4,64,128]{2,1,0:T(8,128)} %source.1), custom_call_target="tpu_custom_call" | custom-call | tf_op jit(solution)/shard_map/mcmc_step/pallas_call | solution.py:454
  49.2 1.6 %copy.7 = f32[1,4,64,128]{3,2,1,0:T(8,128)} copy(f32[1,4,64,128]{3,2,1,0:T(8,128)} %bitcast.3) | data formatting | bytes 262144

commit v2 on v1

--- a/solution.py
+++ b/solution.py
@@ -68,39 +68,101 @@
     return jnp.where(iota(v.shape, 1) < 64, down(swapped, 0, 32), swapped)
 
 
+def xup2(v):
+    moved = up(v, 1, 32)
+    return jnp.where(iota(v.shape, 1) < 96, moved, up(moved, 0))
+
+
+def xdown2(v):
+    moved = down(v, 1, 32)
+    return jnp.where(iota(v.shape, 1) < 32, down(moved, 0), moved)
+
+
 def zup2(v):
-    moved = up(v, 1, 32)
-    return jnp.where(iota(v.shape, 1) < 96, moved, up(moved, 0, 16))
+    return up(v, 0, 4)
 
 
 def zdown2(v):
-    moved = down(v, 1, 32)
-    return jnp.where(iota(v.shape, 1) < 32, down(moved, 0, 16), moved)
-
-
-def flat_coefs(perm, scale, nx, ny, zup, zdown, top):
-    x = lax.rem(iota(perm.shape, 0), nx)
-    y = lax.rem(iota(perm.shape, 1), ny)
-    east = jnp.where(x < nx - 1, scale * harmonic(perm, up(perm, 0)), 0.0)
+    return down(v, 0, 4)
+
+
+def xup1(v):
+    return up(v, 0)
+
+
+def xdown1(v):
+    return down(v, 0)
+
+
+MOVES1 = (xdown1, xup1, zdown1, zup1)
+MOVES2 = (xdown2, xup2, zdown2, zup2)
+
+
+def flat_coefs(perm, scale, x, y, nx, ny, moves, top):
+    xdown, xup, zdown, zup = moves
+    east = jnp.where(x < nx - 1, scale * harmonic(perm, xup(perm)), 0.0)
     north = jnp.where(y < ny - 1, scale * harmonic(perm, up(perm, 1)), 0.0)
     above = jnp.where(top, 0.0, (16.0 * scale) * harmonic(perm, zup(perm)))
-    west, south, below = down(east, 0), down(north, 1), zdown(above)
+    west, south, below = xdown(east), down(north, 1), zdown(above)
     edges = jnp.where(x == 0, scale, 0.0) + jnp.where(x == nx - 1, scale, 0.0)
     edges = edges + jnp.where(y == 0, scale, 0.0) + jnp.where(y == ny - 1, scale, 0.0)
     diag = west + east + south + north + below + above + edges * perm
     return west, east, south, north, below, above, diag, OMEGA / diag
 
 
-def around(v, c, zup, zdown):
-    a = c[0] * down(v, 0) + c[1] * up(v, 0)
+def around(v, c, moves):
+    xdown, xup, zdown, zup = moves
+    a = c[0] * xdown(v) + c[1] * xup(v)
     b = c[2] * down(v, 1) + c[3] * up(v, 1)
     return (a + b) + (c[4] * zdown(v) + c[5] * zup(v))
+
+
+def sweep(v, right, c, moves):
+    return KEEP * v + c[7] * (right + around(v, c, moves))
+
+
+def shifted(pair, parity, offset, cache):
+    dx, dy, dz = offset
+    source = (parity + dz) % 2
+    lanes = dy + 16 * ((parity + dz - source) // 2)
+    if (source, lanes) not in cache:
+        value = pair[source]
+        cache[source, lanes] = value if lanes == 0 else pltpu.roll(value, -lanes % 128, 1)
+    value = cache[source, lanes]
+    return value if dx == 0 else pltpu.roll(value, -dx % 8, 0)
+
+
+def tree_sum(terms):
+    while len(terms) > 1:
+        terms = [a + b for a, b in zip(terms[::2], terms[1::2])] + terms[len(terms) & ~1 :]
+    return terms[0]
+
+
+def apply3(operator, pair, base):
+    cache = {}
+    out = []
+    for parity in range(2):
+        terms = [base[parity]]
+        terms += [c[parity] * shifted(pair, parity, o, cache) for o, c in operator.items()]
+        out.append(tree_sum(terms))
+    return tuple(out)
+
+
+def compose3(first, second):
+    out = {}
+    for o2, c2 in second.items():
+        cache = {}
+        for o1, c1 in first.items():
+            term = [c1[parity] * shifted(c2, parity, o1, cache) for parity in range(2)]
+            key = tuple(a + b for a, b in zip(o1, o2))
+            out[key] = [a + b for a, b in zip(out[key], term)] if key in out else term
+    return out
 
 
 def kernel(
     props, doms, acc_ref, states, noise, source, out_ref,
     rx, cur, nz, perm, src, cw, ce, cs, cn, cu, dg, cc, va, vb, tmp,
-    perm1, right1, tmp1, co1, v1s, tmp2, gp2, gr2, tmp3, e2s,
+    perm1, right1, tmp1, co1, v1s, tmp2, gp2, gr2, co2, m2, tmp3, e2s,
     loc, s1, d1, s2, d2, ss, ds_, sn, dn, sf, df, sq, dq, sp, dp, sr, dr, sg, dgs,
 ):
     me = lax.axis_index("prop")
@@ -149,17 +211,17 @@
         copy.start()
 
     r01, l01 = iota((256, 128), 0), iota((256, 128), 1)
-    c01 = ones_where(l01 == (r01 // 128) * 64 + lax.rem(r01, 128) // 2)
-    r12, l12 = iota((128, 32), 0), iota((128, 32), 1)
-    c12 = ones_where(l12 == lax.rem(r12, 64) // 2)
+    c01 = ones_where(l01 == (r01 >> 1))
+    r12, l12 = iota((512, 128), 0), iota((512, 128), 1)
+    c12 = ones_where(((r12 >> 7) == (l12 >> 5)) & (((r12 & 63) >> 1) == (l12 & 31)))
     r23, l23 = iota((128, 256), 0), iota((128, 256), 1)
-    c23 = ones_where((r23 // 64 == l23 // 128) & (lax.rem(r23, 32) // 2 == lax.rem(l23, 16)))
+    c23 = ones_where(((r23 >> 6) == (l23 >> 7)) & (((r23 & 31) >> 1) == (l23 & 15)))
     r32, l32 = iota((256, 128), 0), iota((256, 128), 1)
-    c32 = ones_where((l32 // 64 == r32 // 128) & (lax.rem(l32, 32) // 2 == lax.rem(r32, 16)))
-    r21, l21 = iota((128, 128), 0), iota((128, 128), 1)
-    c21 = ones_where(lax.rem(l21, 64) // 2 == lax.rem(r21, 32))
+    c32 = ones_where(((l32 >> 6) == (r32 >> 7)) & (((l32 & 31) >> 1) == (r32 & 15)))
+    r21, l21 = iota((128, 512), 0), iota((128, 512), 1)
+    c21 = ones_where(((r21 >> 5) == (l21 >> 7)) & ((r21 & 31) == ((l21 & 63) >> 1)))
     r10, l10 = iota((128, 256), 0), iota((128, 256), 1)
-    c10 = ones_where((r10 // 64 == l10 // 128) & (lax.rem(r10, 64) == lax.rem(l10, 128) // 2))
+    c10 = ones_where(r10 == (l10 >> 1))
     row, lane = iota((64, 128), 0), iota((64, 128), 1)
     east_in, north_in = row < 63, lane < 127
     edges = jnp.where(row == 0, 1.0, 0.0) + jnp.where(row == 63, 1.0, 0.0)
@@ -200,8 +262,12 @@
         return dot3(jnp.concatenate(sums, axis=1), c01)
 
     def restrict12(value):
-        tmp2[pl.ds(0, 32)] = value
-        return dot3(pair_rows(tmp2, 16), c12)
+        tmp2[...] = value
+        parts = []
+        for q in range(4):
+            low = tmp2[pl.ds(2 * q, 4, stride=8), :]
+            parts.append(low + tmp2[pl.ds(2 * q + 1, 4, stride=8), :])
+        return dot3(jnp.concatenate(parts, axis=1), c12)
 
     own1 = 0.125 * restrict01([perm[k] for k in range(4, 8)])
     perm1[3] = own1
@@ -210,8 +276,6 @@
         copy = remote(perm1.at[3], perm1.at[3 - o], sq.at[i], dq.at[i], me, slab(o))
         copy.start()
         sends_q.append(copy)
-    for copy in far:
-        copy.start()
     gp2[dom] = 0.125 * restrict12(own1)
 
     def gather_to(buf, send, recv):
@@ -224,8 +288,6 @@
     def gather_wait(buf, send, recv):
         part = buf.at[pl.ds(0, doms - 1)]
         return remote(part, part, send, recv, me, slab(1))
-
-    gather_to(gp2, sp.at[0], dp.at[0])
 
     def sides(k):
         p = perm[k]
@@ -289,14 +351,34 @@
         copy = remote(right1.at[2], right1.at[2 - o], sr.at[i], dr.at[i], me, slab(o))
         copy.start()
         sends_r.append(copy)
+    for copy in far:
+        copy.start()
+    gather_to(gp2, sp.at[0], dp.at[0])
 
     for copy in sends_q:
         copy.wait_recv()
     wide = perm1[...].reshape(7 * 32, 128)
-    pair = lax.rem(dom + (doms - 3) + iota(wide.shape, 0) // 32, doms)
-    top1 = (pair == doms - 1) & (iota(wide.shape, 1) >= 64)
-    for i, value in enumerate(flat_coefs(wide, 4.0, 32, 64, zup1, zdown1, top1)):
+    wide_row, wide_lane = iota(wide.shape, 0), iota(wide.shape, 1)
+    pair = (dom + (doms - 3) + (wide_row >> 5)) & (doms - 1)
+    top1 = (pair == doms - 1) & (wide_lane >= 64)
+    coefs1 = flat_coefs(wide, 4.0, wide_row & 31, wide_lane & 63, 32, 64, MOVES1, top1)
+    for i, value in enumerate(coefs1):
         co1[i] = value[32:192]
+
+    for copy in sends_r[:2]:
+        copy.wait_recv()
+    b1 = right1[pl.ds(1, 3)].reshape(96, 128)
+    inner = [co1[i, 32:128] for i in range(8)]
+    v1 = sweep(inner[7] * b1, b1, inner, MOVES1)
+    res1 = b1 - inner[6] * v1 + around(v1, inner, MOVES1)
+    gr2[dom] = restrict12(res1[32:64])
+    gather_to(gr2, sg.at[0], dgs.at[0])
+
+    for copy in sends_r[2:]:
+        copy.wait_recv()
+    b1 = right1[...].reshape(160, 128)
+    all1 = [co1[i] for i in range(8)]
+    v1s[...] = sweep(all1[7] * b1, b1, all1, MOVES1)
     for copy in far:
         copy.wait_recv()
     for k in (1, 10):
@@ -308,101 +390,117 @@
     for k in (2, 9):
         vb[k] = sweep0(va, k)
 
-    for copy in sends_r:
-        copy.wait_recv()
-    b1 = right1[...].reshape(160, 128)
-    first = co1[7] * b1
-    v1 = KEEP * first + co1[7] * (b1 + around(first, co1, zup1, zdown1))
-    v1s[...] = v1
-    res1 = b1 - co1[6] * v1 + around(v1, co1, zup1, zdown1)
-    gr2[dom] = restrict12(res1[64:96])
-    gather_to(gr2, sg.at[0], dgs.at[0])
-
-    def whole(buf):
-        groups = []
-        for g in range(doms // 4):
-            groups.append(jnp.concatenate([buf[4 * g + i] for i in range(4)], axis=1))
-        return jnp.concatenate(groups, axis=0)
-
-    rows3, lanes3 = iota((64, 256), 0), iota((64, 256), 1)
-    mask3 = rows3 // 8 == lax.rem(lanes3, 128) // 16
+    row8, row128 = iota((8, 128), 0), iota((128, 128), 0)
+    lane8, lane128 = iota((8, 128), 1), iota((128, 128), 1)
+    group = [(iota((8, 256), 1) & 127) >> 4 == g for g in range(8)]
 
     def restrict23(value):
-        tmp3[...] = value
-        y = jnp.where(mask3, dot3(pair_rows(tmp3, 64), c23), 0.0)
-        total = y[0:8]
-        for g in range(1, 8):
-            total = total + y[8 * g : 8 * g + 8]
-        return total[:, :128], total[:, 128:]
+        both = value + up(value, 0, 4)
+        moved = down(both, 0, 4)
+        parts = []
+        for g in range(8):
+            low, high = both[16 * g : 16 * g + 8], moved[16 * g + 8 : 16 * g + 16]
+            parts.append(jnp.where(row8 < 4, low, high))
+        y = dot3(jnp.concatenate(parts, axis=0), c23)
+        total = tree_sum([jnp.where(group[g], y[8 * g : 8 * g + 8], 0.0) for g in range(8)])
+        for parity in range(2):
+            for q in range(2):
+                piece = total[4 * parity : 4 * parity + 4, 128 * q : 128 * q + 128]
+                tmp3[pl.ds(8 * parity + q, 4, stride=2), :] = piece
+        return tmp3[pl.ds(0, 8), :], tmp3[pl.ds(8, 8), :]
+
+    def prolong23(pair_):
+        tmp3[pl.ds(0, 8), :] = pair_[0]
+        tmp3[pl.ds(8, 8), :] = pair_[1]
+        halves = []
+        for q in range(2):
+            rows = [tmp3[pl.ds(8 * parity + q, 4, stride=2), :] for parity in range(2)]
+            halves.append(jnp.concatenate(rows, axis=0))
+        e = jnp.concatenate(halves, axis=1)
+        y = dot3(jnp.concatenate([jnp.where(m, e, 0.0) for m in group], axis=0), c32)
+        parts = []
+        for g in range(8):
+            value = y[8 * g : 8 * g + 8]
+            other = pltpu.roll(value, 4, 0)
+            parts.append(jnp.where(row8 < 4, value, other))
+            parts.append(jnp.where(row8 < 4, other, value))
+        return jnp.concatenate(parts, axis=0)
 
     gather_wait(gp2, sp.at[0], dp.at[0]).wait_recv()
-    p2 = whole(gp2)
-    top2 = (iota(p2.shape, 0) >= 112) & (iota(p2.shape, 1) >= 96)
-    co2 = flat_coefs(p2, 16.0, 16, 32, zup2, zdown2, top2)
+    p2 = gp2[...].reshape(128, 128)
+    x2 = 4 * (row128 & 3) + (lane128 >> 5)
+    coefs2 = flat_coefs(p2, 16.0, x2, lane128 & 31, 16, 32, MOVES2, row128 >= 124)
+    for i, value in enumerate(coefs2):
+        co2[i] = value
     pa, pb = restrict23(p2)
     pa, pb = 0.125 * pa, 0.125 * pb
-    x3, lane3 = iota((8, 128), 0), iota((8, 128), 1)
-    y3 = lax.rem(lane3, 16)
+    y3 = lane8 & 15
     scale = 64.0
-    edges3 = jnp.where(x3 == 0, scale, 0.0) + jnp.where(x3 == 7, scale, 0.0)
+    edges3 = jnp.where(row8 == 0, scale, 0.0) + jnp.where(row8 == 7, scale, 0.0)
     edges3 = edges3 + jnp.where(y3 == 0, scale, 0.0) + jnp.where(y3 == 15, scale, 0.0)
 
     def sides3(p):
-        east = jnp.where(x3 < 7, scale * harmonic(p, up(p, 0)), 0.0)
+        east = jnp.where(row8 < 7, scale * harmonic(p, up(p, 0)), 0.0)
         north = jnp.where(y3 < 15, scale * harmonic(p, up(p, 1)), 0.0)
         return [down(east, 0), east, down(north, 1), north]
 
     mid = (16.0 * scale) * harmonic(pa, pb)
-    high = jnp.where(lane3 < 112, (16.0 * scale) * harmonic(pb, up(pa, 1, 16)), 0.0)
+    high = jnp.where(lane8 < 112, (16.0 * scale) * harmonic(pb, up(pa, 1, 16)), 0.0)
     low = down(high, 1, 16)
     ca = sides3(pa) + [low, mid]
     cb = sides3(pb) + [mid, high]
 
     def scaled3(c, p):
-        inverse = OMEGA / ((c[0] + c[1]) + (c[2] + c[3]) + (c[4] + c[5]) + edges3 * p)
+        total = (c[0] + c[1]) + (c[2] + c[3]) + (c[4] + c[5]) + edges3 * p
+        inverse = OMEGA / total
         return inverse, [inverse * value for value in c]
 
     ia, ca = scaled3(ca, pa)
     ib, cb = scaled3(cb, pb)
+    keep = jnp.full((8, 128), KEEP, F32)
+    offsets = ((-1, 0, 0), (1, 0, 0), (0, -1, 0), (0, 1, 0), (0, 0, -1), (0, 0, 1))
+    once = {(0, 0, 0): (keep, keep)}
+    once.update({o: (a, b) for o, a, b in zip(offsets, ca, cb)})
+    twice = compose3(once, once)
+    keys = list(twice)
+    for i, key in enumerate(keys):
+        for parity in range(2):
+            m2[parity, i] = twice[key][parity]
 
     gather_wait(gr2, sg.at[0], dgs.at[0]).wait_recv()
-    b2 = whole(gr2)
-    first = co2[7] * b2
-    v2 = KEEP * first + co2[7] * (b2 + around(first, co2, zup2, zdown2))
-    res2 = b2 - co2[6] * v2 + around(v2, co2, zup2, zdown2)
+    b2 = gr2[...].reshape(128, 128)
+    all2 = [co2[i] for i in range(8)]
+    v2 = sweep(all2[7] * b2, b2, all2, MOVES2)
+    res2 = b2 - all2[6] * v2 + around(v2, all2, MOVES2)
     ra, rb = restrict23(res2)
-    ga, gb = ia * ra, ib * rb
-
-    def near3(v, c, base):
-        a = c[0] * down(v, 0) + c[1] * up(v, 0)
-        b = c[2] * down(v, 1) + c[3] * up(v, 1)
-        return (a + b) + (KEEP * v + base)
-
-    def coarse(step, pair_):
-        a, b = pair_
-        new_a = near3(a, ca, ga) + (ca[4] * down(b, 1, 16) + ca[5] * b)
-        new_b = near3(b, cb, gb) + (cb[4] * a + cb[5] * up(a, 1, 16))
-        return new_a, new_b
-
-    ea, eb = lax.fori_loop(0, COARSE_SWEEPS - 1, coarse, (ga, gb))
-    e3 = jnp.concatenate([jnp.concatenate([ea, eb], axis=1)] * 8, axis=0)
-    repeat_rows(tmp3, dot3(jnp.where(mask3, e3, 0.0), c32))
-    v2 = v2 + tmp3[...]
+    base = (ia * ra, ib * rb)
+    base = apply3(once, base, base)
+
+    def coarse(step, value):
+        operator = {key: (m2[0, i], m2[1, i]) for i, key in enumerate(keys)}
+        return apply3(operator, value, base)
+
+    v2 = v2 + prolong23(lax.fori_loop(0, (COARSE_SWEEPS - 2) // 2, coarse, base))
     for _ in range(2):
-        v2 = KEEP * v2 + co2[7] * (b2 + around(v2, co2, zup2, zdown2))
+        v2 = sweep(v2, b2, all2, MOVES2)
     e2s[...] = v2
 
     parts = []
-    lane2 = iota((16, 128), 1) // 32
     for j in range(-2, 3):
         z = slab(j)
-        value = e2s[pl.ds(pl.multiple_of((z // 4) * 16, 16), 16), :]
-        parts.append(jnp.where(lane2 == lax.rem(z, 4), value, 0.0))
-    repeat_rows(tmp1, dot3(jnp.concatenate(parts, axis=0), c21))
+        value = e2s[pl.ds(pl.multiple_of((z // 2) * 8, 8), 8), :]
+        parts.append(jnp.where(lax.rem(z, 2) == 0, value, pltpu.roll(value, 4, 0)))
+    wide1 = dot3(jnp.concatenate(parts, axis=0), c21)
+    for j in range(5):
+        for q in range(4):
+            piece = wide1[8 * j : 8 * j + 4, 128 * q : 128 * q + 128]
+            for i in range(2):
+                tmp1[pl.ds(32 * j + 2 * q + i, 4, stride=8), :] = piece
     v1 = v1s[...] + tmp1[...]
     b1 = right1[...].reshape(160, 128)
+    all1 = [co1[i] for i in range(8)]
     for _ in range(2):
-        v1 = KEEP * v1 + co1[7] * (b1 + around(v1, co1, zup1, zdown1))
+        v1 = sweep(v1, b1, all1, MOVES1)
 
     fine = dot3(v1[32:128], c10)
     for k, i, half in ((2, 0, 1), (4, 1, 0), (6, 1, 1), (8, 2, 0)):
@@ -441,9 +539,11 @@
         pltpu.VMEM((8, 160, 128), F32),
         pltpu.VMEM((160, 128), F32),
         pltpu.VMEM((32, 128), F32),
-        pltpu.VMEM((doms, 16, 32), F32),
-        pltpu.VMEM((doms, 16, 32), F32),
-        pltpu.VMEM((128, 128), F32),
+        pltpu.VMEM((doms, 4, 128), F32),
+        pltpu.VMEM((doms, 4, 128), F32),
+        pltpu.VMEM((8, 128, 128), F32),
+        pltpu.VMEM((2, 25, 8, 128), F32),
+        pltpu.VMEM((16, 128), F32),
         pltpu.VMEM((128, 128), F32),
         dma((3,)),
         dma((props - 1,)), dma((props - 1,)), dma((props - 1,)), dma((props - 1,)),

time: 50.9 us -> 42.8 us (0.84)
  Pallas kernels: 48.5 us -> 40 us
    pallas_call x1, Pallas kernels: 48.5 us -> 40 us  [body(): pl.pallas_call(functools.partial(kernel, props, doms), out_shape=jax.Shap...]
where the time goes in v2:
time: 42.8 us; the launch traced here: 42.2 us
  Pallas kernels  40 us (93%)
  local copies, waits for them, and re-layouts  1.57 us (4%)
  between operations  0.66 us (2%)
    pallas_call x1, Pallas kernels, body(): pl.pallas_call(functools.partial(kernel, props, doms), out_shape=jax.Shap...  40 us
    unnamed x1, local copies, waits for them, and re-layouts  1.57 us

profile of v2, /device:TPU:1, one launch (start us, length us, event | category | flops | bytes accessed | tf_op | source)
XLA Modules:
  0.0 42.2 jit_solution(13809172991402599603)
XLA Ops:
  0.7 40.0 %mcmc_step.1 = f32[4,64,128]{2,1,0:T(8,128)} custom-call(s32[1]{0:T(128)S(6)} %copy.6.acc_ref, f32[8,32,128]{2,1,0:T(8,128)} %bitcast.4, f32[8,32,128]{2,1,0:T(8,128)} %bitcast.5, f32[4,64,128]{2,1,0:T(8,128)} %source.1), custom_call_target="tpu_custom_call" | custom-call | tf_op jit(solution)/shard_map/mcmc_step/pallas_call | solution.py:554
  40.6 1.6 %copy.7 = f32[1,4,64,128]{3,2,1,0:T(8,128)} copy(f32[1,4,64,128]{3,2,1,0:T(8,128)} %bitcast.3) | data formatting | bytes 262144

commit v3 on v2

--- a/solution.py
+++ b/solution.py
@@ -163,10 +163,12 @@
     props, doms, acc_ref, states, noise, source, out_ref,
     rx, cur, nz, perm, src, cw, ce, cs, cn, cu, dg, cc, va, vb, tmp,
     perm1, right1, tmp1, co1, v1s, tmp2, gp2, gr2, co2, m2, tmp3, e2s,
-    loc, s1, d1, s2, d2, ss, ds_, sn, dn, sf, df, sq, dq, sp, dp, sr, dr, sg, dgs,
+    loc, s1, d1, s2, d2, ss, ds_, sn, dn, sf, df, sq, dq, sp, dp, sr, dr, sg, dgs, word,
 ):
     me = lax.axis_index("prop")
     dom = lax.axis_index("dom")
+
+    peers = sorted(range(1, props), key=lambda o: -min(o, props - o))
 
     def peer(o):
         return lax.rem(me + o, props)
@@ -191,15 +193,25 @@
     for o in range(1, props):
         pl.semaphore_signal(barrier, inc=1, device_id=(peer(o), dom), device_id_type=MESH)
 
-    def greet(o, carry):
+    for o in (1, -1, 2, -2, 3, -3):
         pl.semaphore_signal(barrier, inc=1, device_id=(me, slab(o)), device_id_type=MESH)
-        return carry
-
-    lax.fori_loop(1, doms, greet, 0)
-    pl.semaphore_wait(barrier, props + doms - 2)
+    pl.semaphore_wait(barrier, props + 5)
+
+    reach = (3, 6, 12)
+
+    def tell(i):
+        for side, o in enumerate((reach[i], -reach[i])):
+            target = (me, slab(o))
+            pl.semaphore_signal(word.at[i, side], inc=1, device_id=target, device_id_type=MESH)
+
+    def hear(i):
+        for side in range(2):
+            pl.semaphore_wait(word.at[i, side], 1)
+
+    tell(0)
 
     sends1 = []
-    for o in range(1, props):
+    for o in peers:
         copy = remote(states.at[peer(o)], rx.at[me], s1.at[o - 1], d1.at[o - 1], peer(o), dom)
         copy.start()
         sends1.append(copy)
@@ -207,8 +219,6 @@
         remote(source, src.at[pl.ds(0, 4)], ss.at[0], ds_.at[0], me, slab(1)),
         remote(source, src.at[pl.ds(8, 4)], ss.at[1], ds_.at[1], me, slab(-1)),
     ]
-    for copy in sends_src:
-        copy.start()
 
     r01, l01 = iota((256, 128), 0), iota((256, 128), 1)
     c01 = ones_where(l01 == (r01 >> 1))
@@ -231,28 +241,40 @@
     for copy in sends1:
         copy.wait_recv()
     cur[me] = rx[acc_ref[0]]
-    sends2 = []
-    for o in range(1, props):
+    hear(0)
+    tell(1)
+    sends2 = {}
+    for o in peers:
         copy = remote(cur.at[me], cur.at[me], s2.at[o - 1], d2.at[o - 1], peer(o), dom)
         copy.start()
-        sends2.append(copy)
+        sends2[o] = copy
+    for copy in sends_src:
+        copy.start()
     load_noise.wait()
-    for copy in sends2:
-        copy.wait_recv()
-
-    theta = SHRINK * cur[...] + BETA * nz[...]
-    perm[pl.ds(4, 4)] = jnp.exp(theta).reshape(4, 64, 128)
-
+    hear(1)
+    tell(2)
+
+    per_plane = 64 // cur.shape[1]
+    for o in [0] + peers[::-1]:
+        if o:
+            sends2[o].wait_recv()
+        j = peer(-o + props)
+        rows = pl.ds(pl.multiple_of(lax.rem(j, per_plane) * cur.shape[1], 32), cur.shape[1])
+        plane = j // per_plane
+        perm[4 + plane, rows] = jnp.exp(SHRINK * cur[j] + BETA * nz[j])
+        here = perm.at[4 + plane, rows]
+        low, high = (plane == 0).astype(jnp.int32), (plane == 3).astype(jnp.int32)
+        remote(here, perm.at[plane, rows], sn.at[low], dn.at[low], me, slab(1)).start()
+        remote(here, perm.at[8 + plane, rows], sf.at[high], df.at[high], me, slab(-1)).start()
+    sends2 = [sends2[o] for o in peers]
     near = [
         remote(perm.at[pl.ds(5, 3)], perm.at[pl.ds(1, 3)], sn.at[0], dn.at[0], me, slab(1)),
-        remote(perm.at[pl.ds(4, 3)], perm.at[pl.ds(8, 3)], sn.at[1], dn.at[1], me, slab(-1)),
+        remote(perm.at[pl.ds(4, 3)], perm.at[pl.ds(8, 3)], sf.at[0], df.at[0], me, slab(-1)),
     ]
     far = [
-        remote(perm.at[4], perm.at[0], sf.at[0], df.at[0], me, slab(1)),
+        remote(perm.at[4], perm.at[0], sn.at[1], dn.at[1], me, slab(1)),
         remote(perm.at[7], perm.at[11], sf.at[1], df.at[1], me, slab(-1)),
     ]
-    for copy in near:
-        copy.start()
 
     def restrict01(planes):
         sums = []
@@ -279,15 +301,19 @@
     gp2[dom] = 0.125 * restrict12(own1)
 
     def gather_to(buf, send, recv):
-        def go(o, carry):
-            remote(buf.at[dom], buf.at[dom], send, recv, me, slab(o)).start()
+        def go(i, carry):
+            step = (i + 1) // 2 * (2 * lax.rem(i, 2) - 1)
+            remote(buf.at[dom], buf.at[dom], send, recv, me, slab(doms // 2 + step)).start()
             return carry
 
-        lax.fori_loop(1, doms, go, 0)
+        lax.fori_loop(0, doms - 1, go, 0)
 
     def gather_wait(buf, send, recv):
         part = buf.at[pl.ds(0, doms - 1)]
         return remote(part, part, send, recv, me, slab(1))
+
+    hear(2)
+    gather_to(gp2, sp.at[0], dp.at[0])
 
     def sides(k):
         p = perm[k]
@@ -351,9 +377,6 @@
         copy = remote(right1.at[2], right1.at[2 - o], sr.at[i], dr.at[i], me, slab(o))
         copy.start()
         sends_r.append(copy)
-    for copy in far:
-        copy.start()
-    gather_to(gp2, sp.at[0], dp.at[0])
 
     for copy in sends_q:
         copy.wait_recv()
@@ -549,11 +572,12 @@
         dma((props - 1,)), dma((props - 1,)), dma((props - 1,)), dma((props - 1,)),
         dma((2,)), dma((2,)), dma((2,)), dma((2,)), dma((2,)), dma((2,)),
         dma((6,)), dma((6,)), dma((1,)), dma((1,)), dma((4,)), dma((4,)), dma((1,)), dma((1,)),
+        pltpu.SemaphoreType.REGULAR((3, 2)),
     ]
     hbm = pl.BlockSpec(memory_space=pl.ANY)
     out = pl.pallas_call(
         functools.partial(kernel, props, doms),
-        out_shape=jax.ShapeDtypeStruct((4, 64, 128), F32),
+        out_shape=pltpu.VMEM((4, 64, 128), F32),
         in_specs=[pl.BlockSpec(memory_space=pltpu.SMEM), hbm, hbm, hbm],
         out_specs=pl.BlockSpec(memory_space=pltpu.VMEM),
         scratch_shapes=scratch,

time: 42.8 us -> 40 us (0.935)
  the two profiles are of different devices: /device:TPU:1 before, /device:TPU:32 now
where the time goes in v3:
time: 40 us
  Pallas kernels  38.6 us (96%)
  local copies, waits for them, and re-layouts  0.66 us (2%)
  between operations  0.66 us (2%)
    pallas_call x1, Pallas kernels, body(): pl.pallas_call(functools.partial(kernel, props, doms), out_shape=pltpu.VM...  38.6 us

profile of v3, /device:TPU:32, one launch (start us, length us, event | category | flops | bytes accessed | tf_op | source)
XLA Modules:
  0.0 40.0 jit_solution(15427174514891822107)
XLA Ops:
  0.7 38.6 %mcmc_step.1 = f32[4,64,128]{2,1,0:T(8,128)S(1)} custom-call(s32[1]{0:T(128)S(6)} %copy.7.acc_ref, f32[8,32,128]{2,1,0:T(8,128)} %bitcast.4, f32[8,32,128]{2,1,0:T(8,128)} %bitcast.5, f32[4,64,128]{2,1,0:T(8,128)} %source.1), custom_call_target="tpu_custom_call" | custom-call | tf_op jit(solution)/shard_map/mcmc_step/pallas_call | solution.py:578
  39.3 0.7 %copy.6 = f32[1,4,64,128]{3,2,1,0:T(8,128)} copy(f32[1,4,64,128]{3,2,1,0:T(8,128)S(1)} %bitcast.3) | data formatting | bytes 262144

commit v4 on v3

--- a/solution.py
+++ b/solution.py
@@ -160,18 +160,16 @@
 
 
 def kernel(
-    props, doms, acc_ref, states, noise, source, out_ref,
-    rx, cur, nz, perm, src, cw, ce, cs, cn, cu, dg, cc, va, vb, tmp,
+    props, doms, root, states, noise, source, out_ref,
+    cur, nz, perm, src, cw, ce, cs, cn, cu, dg, cc, va, vb, tmp,
     perm1, right1, tmp1, co1, v1s, tmp2, gp2, gr2, co2, m2, tmp3, e2s,
-    loc, s1, d1, s2, d2, ss, ds_, sn, dn, sf, df, sq, dq, sp, dp, sr, dr, sg, dgs, word,
+    loc, s1, d1, ss, ds_, sn, dn, sf, df, sq, dq, sp, dp, sr, dr, sg, dgs, word,
 ):
     me = lax.axis_index("prop")
     dom = lax.axis_index("dom")
 
-    peers = sorted(range(1, props), key=lambda o: -min(o, props - o))
-
-    def peer(o):
-        return lax.rem(me + o, props)
+    spread = lambda p: -min((p - root) % props, (root - p) % props)
+    peers = sorted((p for p in range(props) if p != root), key=spread)
 
     def slab(o):
         return lax.rem(dom + (o + doms), doms)
@@ -184,18 +182,29 @@
 
     load_noise = pltpu.make_async_copy(noise, nz, loc.at[0])
     load_source = pltpu.make_async_copy(source, src.at[pl.ds(4, 4)], loc.at[1])
-    load_piece = pltpu.make_async_copy(states.at[me], rx.at[me], loc.at[2])
-    load_piece.start()
     load_noise.start()
     load_source.start()
+    order = (1, 2, 3, 0)
+
+    def load_plane(k):
+        return pltpu.make_async_copy(states.at[k], cur.at[k], d1.at[k])
 
     barrier = pltpu.get_barrier_semaphore()
-    for o in range(1, props):
-        pl.semaphore_signal(barrier, inc=1, device_id=(peer(o), dom), device_id_type=MESH)
+
+    @pl.when(me != root)
+    def _():
+        pl.semaphore_signal(barrier, inc=1, device_id=(root, dom), device_id_type=MESH)
 
     for o in (1, -1, 2, -2, 3, -3):
         pl.semaphore_signal(barrier, inc=1, device_id=(me, slab(o)), device_id_type=MESH)
-    pl.semaphore_wait(barrier, props + 5)
+    pl.semaphore_wait(barrier, jnp.where(me == root, props + 5, 6))
+
+    @pl.when(me == root)
+    def _():
+        for k in order:
+            for p in peers:
+                remote(states.at[k], cur.at[k], s1.at[p], d1.at[k], p, dom).start()
+            load_plane(k).start()
 
     reach = (3, 6, 12)
 
@@ -210,15 +219,12 @@
 
     tell(0)
 
-    sends1 = []
-    for o in peers:
-        copy = remote(states.at[peer(o)], rx.at[me], s1.at[o - 1], d1.at[o - 1], peer(o), dom)
-        copy.start()
-        sends1.append(copy)
     sends_src = [
         remote(source, src.at[pl.ds(0, 4)], ss.at[0], ds_.at[0], me, slab(1)),
         remote(source, src.at[pl.ds(8, 4)], ss.at[1], ds_.at[1], me, slab(-1)),
     ]
+    for copy in sends_src:
+        copy.start()
 
     r01, l01 = iota((256, 128), 0), iota((256, 128), 1)
     c01 = ones_where(l01 == (r01 >> 1))
@@ -237,36 +243,18 @@
     edges = jnp.where(row == 0, 1.0, 0.0) + jnp.where(row == 63, 1.0, 0.0)
     edges = edges + jnp.where(lane == 0, 1.0, 0.0) + jnp.where(lane == 127, 1.0, 0.0)
 
-    load_piece.wait()
-    for copy in sends1:
-        copy.wait_recv()
-    cur[me] = rx[acc_ref[0]]
+    load_noise.wait()
     hear(0)
     tell(1)
-    sends2 = {}
-    for o in peers:
-        copy = remote(cur.at[me], cur.at[me], s2.at[o - 1], d2.at[o - 1], peer(o), dom)
-        copy.start()
-        sends2[o] = copy
-    for copy in sends_src:
-        copy.start()
-    load_noise.wait()
+    for k in order:
+        load_plane(k).wait()
+        perm[4 + k] = jnp.exp(SHRINK * cur[k] + BETA * nz[k])
+        low, high = int(k == 0), int(k == 3)
+        here = perm.at[4 + k]
+        remote(here, perm.at[k], sn.at[low], dn.at[low], me, slab(1)).start()
+        remote(here, perm.at[8 + k], sf.at[high], df.at[high], me, slab(-1)).start()
     hear(1)
     tell(2)
-
-    per_plane = 64 // cur.shape[1]
-    for o in [0] + peers[::-1]:
-        if o:
-            sends2[o].wait_recv()
-        j = peer(-o + props)
-        rows = pl.ds(pl.multiple_of(lax.rem(j, per_plane) * cur.shape[1], 32), cur.shape[1])
-        plane = j // per_plane
-        perm[4 + plane, rows] = jnp.exp(SHRINK * cur[j] + BETA * nz[j])
-        here = perm.at[4 + plane, rows]
-        low, high = (plane == 0).astype(jnp.int32), (plane == 3).astype(jnp.int32)
-        remote(here, perm.at[plane, rows], sn.at[low], dn.at[low], me, slab(1)).start()
-        remote(here, perm.at[8 + plane, rows], sf.at[high], df.at[high], me, slab(-1)).start()
-    sends2 = [sends2[o] for o in peers]
     near = [
         remote(perm.at[pl.ds(5, 3)], perm.at[pl.ds(1, 3)], sn.at[0], dn.at[0], me, slab(1)),
         remote(perm.at[pl.ds(4, 3)], perm.at[pl.ds(8, 3)], sf.at[0], df.at[0], me, slab(-1)),
@@ -536,7 +524,12 @@
     for k in range(4, 8):
         out_ref[k - 4] = sweep0(va, k)
 
-    for copies in (sends1, sends2, sends_src, near, far, sends_q, sends_r):
+    @pl.when(me == root)
+    def _():
+        for p in peers:
+            remote(cur, cur, s1.at[p], d1.at[0], p, dom).wait_send()
+
+    for copies in (sends_src, near, far, sends_q, sends_r):
         for copy in copies:
             copy.wait_send()
     gather_wait(gp2, sp.at[0], dp.at[0]).wait_send()
@@ -545,13 +538,10 @@
 
 def body(states, accepted, noise, source):
     props, doms = lax.axis_size("prop"), lax.axis_size("dom")
-    rows = 256 // props
     dma = pltpu.SemaphoreType.DMA
     plane = lambda n: pltpu.VMEM((n, 64, 128), F32)
     scratch = [
-        pltpu.VMEM((props, rows, 128), F32),
-        pltpu.VMEM((props, rows, 128), F32),
-        pltpu.VMEM((props, rows, 128), F32),
+        plane(4), plane(4),
         plane(12), plane(12),
         plane(12), plane(12), plane(12), plane(12), plane(12), plane(12), plane(12),
         plane(12), plane(12),
@@ -568,28 +558,26 @@
         pltpu.VMEM((2, 25, 8, 128), F32),
         pltpu.VMEM((16, 128), F32),
         pltpu.VMEM((128, 128), F32),
-        dma((3,)),
-        dma((props - 1,)), dma((props - 1,)), dma((props - 1,)), dma((props - 1,)),
+        dma((2,)), dma((props,)), dma((4,)),
         dma((2,)), dma((2,)), dma((2,)), dma((2,)), dma((2,)), dma((2,)),
         dma((6,)), dma((6,)), dma((1,)), dma((1,)), dma((4,)), dma((4,)), dma((1,)), dma((1,)),
         pltpu.SemaphoreType.REGULAR((3, 2)),
     ]
     hbm = pl.BlockSpec(memory_space=pl.ANY)
-    out = pl.pallas_call(
-        functools.partial(kernel, props, doms),
-        out_shape=pltpu.VMEM((4, 64, 128), F32),
-        in_specs=[pl.BlockSpec(memory_space=pltpu.SMEM), hbm, hbm, hbm],
-        out_specs=pl.BlockSpec(memory_space=pltpu.VMEM),
-        scratch_shapes=scratch,
-        compiler_params=pltpu.CompilerParams(collective_id=0, has_side_effects=True),
-        name="mcmc_step",
-    )(
-        accepted,
-        states.reshape(props, rows, 128),
-        noise.reshape(props, rows, 128),
-        source,
-    )
-    return out[None]
+
+    def branch(root):
+        return pl.pallas_call(
+            functools.partial(kernel, props, doms, root),
+            out_shape=pltpu.VMEM((4, 64, 128), F32),
+            in_specs=[hbm, hbm, hbm],
+            out_specs=pl.BlockSpec(memory_space=pltpu.VMEM),
+            scratch_shapes=scratch,
+            compiler_params=pltpu.CompilerParams(collective_id=root, has_side_effects=True),
+            name=f"mcmc_step_{root}",
+        )
+
+    branches = [branch(root) for root in range(props)]
+    return lax.switch(accepted[0], branches, states[0], noise[0], source)[None]
 
 
 def solution(mesh):

time: 40 us -> 37.5 us (0.938)
  the two profiles are of different devices: /device:TPU:32 before, /device:TPU:8 now
where the time goes in v4:
time: 37.5 us; the launch traced here: 37.4 us
  Pallas kernels  35.5 us (95%)
  local copies, waits for them, and re-layouts  0.66 us (2%)
  between operations  0.66 us (2%)
  loops' own time  0.57 us (2%)
    pallas_call x1, Pallas kernels, body(): return lax.switch(accepted[0], branches, states[0], noise[0], source)[None]  35.5 us

profile of v4, /device:TPU:8, one launch (start us, length us, event | category | flops | bytes accessed | tf_op | source)
XLA Modules:
  0.0 37.4 jit_solution(16114842497255451605)
XLA Ops:
  0.7 36.0 %conditional.1 = (f32[1,4,64,128]{3,2,1,0:T(8,128)S(1)}) conditional(s32[]{:T(128)} %bitcast.8, (f32[4,64,128]{2,1,0:T(8,128)}, f32[4,64,128]{2,1,0:T(8,128)}, f32[4,64,128]{2,1,0:T(8,128)}) %tuple.62, (f32[4,64,128]{2,1,0:T(8,128)}, f32[4,64,128]{2,1,0:T(8,128)}, f32[4,64,128]{2,1,0:T(8,128)}) %tuple.63, ...), branch_computations={%region_0.0_spmd, %region_1.0_spmd, %region_2.0_spmd, %region_3.0_... | conditional | bytes 8 | solution.py:580
  0.9 35.5 %mcmc_step_5.1 = f32[4,64,128]{2,1,0:T(8,128)S(1)} custom-call(f32[4,64,128]{2,1,0:T(8,128)} %get-tuple-element.78.states, f32[4,64,128]{2,1,0:T(8,128)} %get-tuple-element.79.noise, f32[4,64,128]{2,1,0:T(8,128)} %get-tuple-element.80.source), custom_call_target="tpu_custom_call" | custom-call | tf_op jit(solution)/shard_map/cond/branch_5_fun/mcmc_step_5/pallas_call | solution.py:580
  36.7 0.7 %copy.22 = f32[1,4,64,128]{3,2,1,0:T(8,128)} copy(f32[1,4,64,128]{3,2,1,0:T(8,128)S(1)} %get-tuple-element.87) | data formatting | bytes 262144

commit v5 on v4

--- a/solution.py
+++ b/solution.py
@@ -162,8 +162,8 @@
 def kernel(
     props, doms, root, states, noise, source, out_ref,
     cur, nz, perm, src, cw, ce, cs, cn, cu, dg, cc, va, vb, tmp,
-    perm1, right1, tmp1, co1, v1s, tmp2, gp2, gr2, co2, m2, tmp3, e2s,
-    loc, s1, d1, ss, ds_, sn, dn, sf, df, sq, dq, sp, dp, sr, dr, sg, dgs, word,
+    perm1, right1, tmp1, co1, v1s, tmp2, gp2, gr2, co2, m3, tmp3, e2s,
+    loc, s1, d1, s2, ss, ds_, sn, dn, sf, df, sq, dq, sp, dp, sr, dr, sg, dgs, word,
 ):
     me = lax.axis_index("prop")
     dom = lax.axis_index("dom")
@@ -195,15 +195,24 @@
     def _():
         pl.semaphore_signal(barrier, inc=1, device_id=(root, dom), device_id_type=MESH)
 
+    mate = me + 1 - 2 * lax.rem(me, 2)
+    away = me // 2 != root // 2
+
+    @pl.when(away)
+    def _():
+        pl.semaphore_signal(barrier, inc=1, device_id=(mate, dom), device_id_type=MESH)
+
     for o in (1, -1, 2, -2, 3, -3):
         pl.semaphore_signal(barrier, inc=1, device_id=(me, slab(o)), device_id_type=MESH)
-    pl.semaphore_wait(barrier, jnp.where(me == root, props + 5, 6))
+    extra = jnp.where(me == root, props - 1, jnp.where(away, 1, 0))
+    pl.semaphore_wait(barrier, 6 + extra)
 
     @pl.when(me == root)
     def _():
         for k in order:
             for p in peers:
-                remote(states.at[k], cur.at[k], s1.at[p], d1.at[k], p, dom).start()
+                if p // 2 == root // 2 or p % 2 == k % 2:
+                    remote(states.at[k], cur.at[k], s1.at[p, k], d1.at[k], p, dom).start()
             load_plane(k).start()
 
     reach = (3, 6, 12)
@@ -248,11 +257,17 @@
     tell(1)
     for k in order:
         load_plane(k).wait()
+
+        @pl.when(away & (lax.rem(me, 2) == k % 2))
+        def _(k=k):
+            remote(cur.at[k], cur.at[k], s2.at[k], d1.at[k], mate, dom).start()
+
         perm[4 + k] = jnp.exp(SHRINK * cur[k] + BETA * nz[k])
-        low, high = int(k == 0), int(k == 3)
         here = perm.at[4 + k]
-        remote(here, perm.at[k], sn.at[low], dn.at[low], me, slab(1)).start()
-        remote(here, perm.at[8 + k], sf.at[high], df.at[high], me, slab(-1)).start()
+        if k > 0:
+            remote(here, perm.at[k], sn.at[0], dn.at[0], me, slab(1)).start()
+        if k < 3:
+            remote(here, perm.at[8 + k], sf.at[0], df.at[0], me, slab(-1)).start()
     hear(1)
     tell(2)
     near = [
@@ -263,6 +278,8 @@
         remote(perm.at[4], perm.at[0], sn.at[1], dn.at[1], me, slab(1)),
         remote(perm.at[7], perm.at[11], sf.at[1], df.at[1], me, slab(-1)),
     ]
+    for copy in far:
+        copy.start()
 
     def restrict01(planes):
         sums = []
@@ -472,11 +489,11 @@
     offsets = ((-1, 0, 0), (1, 0, 0), (0, -1, 0), (0, 1, 0), (0, 0, -1), (0, 0, 1))
     once = {(0, 0, 0): (keep, keep)}
     once.update({o: (a, b) for o, a, b in zip(offsets, ca, cb)})
-    twice = compose3(once, once)
-    keys = list(twice)
+    thrice = compose3(once, compose3(once, once))
+    keys = list(thrice)
     for i, key in enumerate(keys):
         for parity in range(2):
-            m2[parity, i] = twice[key][parity]
+            m3[parity, i] = thrice[key][parity]
 
     gather_wait(gr2, sg.at[0], dgs.at[0]).wait_recv()
     b2 = gr2[...].reshape(128, 128)
@@ -485,13 +502,14 @@
     res2 = b2 - all2[6] * v2 + around(v2, all2, MOVES2)
     ra, rb = restrict23(res2)
     base = (ia * ra, ib * rb)
-    base = apply3(once, base, base)
+    right3 = base
+    base = apply3(once, apply3(once, right3, right3), right3)
 
     def coarse(step, value):
-        operator = {key: (m2[0, i], m2[1, i]) for i, key in enumerate(keys)}
+        operator = {key: (m3[0, i], m3[1, i]) for i, key in enumerate(keys)}
         return apply3(operator, value, base)
 
-    v2 = v2 + prolong23(lax.fori_loop(0, (COARSE_SWEEPS - 2) // 2, coarse, base))
+    v2 = v2 + prolong23(lax.fori_loop(0, (COARSE_SWEEPS - 1) // 3, coarse, right3))
     for _ in range(2):
         v2 = sweep(v2, b2, all2, MOVES2)
     e2s[...] = v2
@@ -526,8 +544,16 @@
 
     @pl.when(me == root)
     def _():
-        for p in peers:
-            remote(cur, cur, s1.at[p], d1.at[0], p, dom).wait_send()
+        for k in order:
+            for p in peers:
+                if p // 2 == root // 2 or p % 2 == k % 2:
+                    remote(states.at[k], cur.at[k], s1.at[p, k], d1.at[k], p, dom).wait_send()
+
+    for k in order:
+
+        @pl.when(away & (lax.rem(me, 2) == k % 2))
+        def _(k=k):
+            remote(cur.at[k], cur.at[k], s2.at[k], d1.at[k], mate, dom).wait_send()
 
     for copies in (sends_src, near, far, sends_q, sends_r):
         for copy in copies:
@@ -555,10 +581,10 @@
         pltpu.VMEM((doms, 4, 128), F32),
         pltpu.VMEM((doms, 4, 128), F32),
         pltpu.VMEM((8, 128, 128), F32),
-        pltpu.VMEM((2, 25, 8, 128), F32),
+        pltpu.VMEM((2, 63, 8, 128), F32),
         pltpu.VMEM((16, 128), F32),
         pltpu.VMEM((128, 128), F32),
-        dma((2,)), dma((props,)), dma((4,)),
+        dma((2,)), dma((props, 4)), dma((4,)), dma((4,)),
         dma((2,)), dma((2,)), dma((2,)), dma((2,)), dma((2,)), dma((2,)),
         dma((6,)), dma((6,)), dma((1,)), dma((1,)), dma((4,)), dma((4,)), dma((1,)), dma((1,)),
         pltpu.SemaphoreType.REGULAR((3, 2)),

time: 37.5 us -> 37.8 us (level)
  the two profiles are of different devices: /device:TPU:8 before, /device:TPU:1 now
where the time goes in v5:
time: 37.8 us; the launch traced here: 37.7 us
  Pallas kernels  35.8 us (95%)
  local copies, waits for them, and re-layouts  0.66 us (2%)
  between operations  0.66 us (2%)
  loops' own time  0.57 us (2%)
    pallas_call x1, Pallas kernels, body(): return lax.switch(accepted[0], branches, states[0], noise[0], source)[None]  35.8 us

profile of v5, /device:TPU:1, one launch (start us, length us, event | category | flops | bytes accessed | tf_op | source)
XLA Modules:
  0.0 37.7 jit_solution(2862374626553958780)
XLA Ops:
  0.7 36.4 %conditional.1 = (f32[1,4,64,128]{3,2,1,0:T(8,128)S(1)}) conditional(s32[]{:T(128)} %bitcast.8, (f32[4,64,128]{2,1,0:T(8,128)}, f32[4,64,128]{2,1,0:T(8,128)}, f32[4,64,128]{2,1,0:T(8,128)}) %tuple.62, (f32[4,64,128]{2,1,0:T(8,128)}, f32[4,64,128]{2,1,0:T(8,128)}, f32[4,64,128]{2,1,0:T(8,128)}) %tuple.63, ...), branch_computations={%region_0.0_spmd, %region_1.0_spmd, %region_2.0_spmd, %region_3.0_... | conditional | bytes 8 | solution.py:606
  0.9 35.8 %mcmc_step_6.1 = f32[4,64,128]{2,1,0:T(8,128)S(1)} custom-call(f32[4,64,128]{2,1,0:T(8,128)} %get-tuple-element.81.states, f32[4,64,128]{2,1,0:T(8,128)} %get-tuple-element.82.noise, f32[4,64,128]{2,1,0:T(8,128)} %get-tuple-element.83.source), custom_call_target="tpu_custom_call" | custom-call | tf_op jit(solution)/shard_map/cond/branch_6_fun/mcmc_step_6/pallas_call | solution.py:606
  37.0 0.7 %copy.22 = f32[1,4,64,128]{3,2,1,0:T(8,128)} copy(f32[1,4,64,128]{3,2,1,0:T(8,128)S(1)} %get-tuple-element.87) | data formatting | bytes 262144

commit v6 on v5

--- a/solution.py
+++ b/solution.py
@@ -163,7 +163,7 @@
     props, doms, root, states, noise, source, out_ref,
     cur, nz, perm, src, cw, ce, cs, cn, cu, dg, cc, va, vb, tmp,
     perm1, right1, tmp1, co1, v1s, tmp2, gp2, gr2, co2, m3, tmp3, e2s,
-    loc, s1, d1, s2, ss, ds_, sn, dn, sf, df, sq, dq, sp, dp, sr, dr, sg, dgs, word,
+    loc, s1, d1, s2, ss, ds_, sn, dn, sf, sq, dq, sp, dp, sr, dr, sg, dgs, word, ready,
 ):
     me = lax.axis_index("prop")
     dom = lax.axis_index("dom")
@@ -191,28 +191,43 @@
 
     barrier = pltpu.get_barrier_semaphore()
 
-    @pl.when(me != root)
+    mate = me + 1 - 2 * lax.rem(me, 2)
+    away = me // 2 != root // 2
+    relay = away & (lax.rem(me, 2) == 0)
+    leads = relay | (me == root)
+
+    @pl.when(relay)
     def _():
         pl.semaphore_signal(barrier, inc=1, device_id=(root, dom), device_id_type=MESH)
 
-    mate = me + 1 - 2 * lax.rem(me, 2)
-    away = me // 2 != root // 2
-
-    @pl.when(away)
+    @pl.when(leads)
     def _():
         pl.semaphore_signal(barrier, inc=1, device_id=(mate, dom), device_id_type=MESH)
 
     for o in (1, -1, 2, -2, 3, -3):
         pl.semaphore_signal(barrier, inc=1, device_id=(me, slab(o)), device_id_type=MESH)
-    extra = jnp.where(me == root, props - 1, jnp.where(away, 1, 0))
+    extra = jnp.where(me == root, props // 2 - 1, jnp.where(leads, 0, 1))
     pl.semaphore_wait(barrier, 6 + extra)
+
+    @pl.when(jnp.logical_not(leads))
+    def _():
+        pl.semaphore_signal(ready, inc=1, device_id=(mate, dom), device_id_type=MESH)
+
+    def across(k):
+        return [
+            remote(states.at[k], cur.at[k], s1.at[p, k], d1.at[k], p, dom)
+            for p in peers
+            if p // 2 != root // 2 and p % 2 == 0
+        ]
+
+    def hand_over(k, from_ref):
+        return remote(from_ref, cur.at[k], s2.at[k], d1.at[k], mate, dom)
 
     @pl.when(me == root)
     def _():
         for k in order:
-            for p in peers:
-                if p // 2 == root // 2 or p % 2 == k % 2:
-                    remote(states.at[k], cur.at[k], s1.at[p, k], d1.at[k], p, dom).start()
+            for copy in across(k):
+                copy.start()
             load_plane(k).start()
 
     reach = (3, 6, 12)
@@ -229,8 +244,8 @@
     tell(0)
 
     sends_src = [
-        remote(source, src.at[pl.ds(0, 4)], ss.at[0], ds_.at[0], me, slab(1)),
-        remote(source, src.at[pl.ds(8, 4)], ss.at[1], ds_.at[1], me, slab(-1)),
+        remote(source.at[pl.ds(1, 3)], src.at[pl.ds(1, 3)], ss.at[0], ds_.at[0], me, slab(1)),
+        remote(source.at[pl.ds(0, 3)], src.at[pl.ds(8, 3)], ss.at[1], ds_.at[1], me, slab(-1)),
     ]
     for copy in sends_src:
         copy.start()
@@ -255,28 +270,35 @@
     load_noise.wait()
     hear(0)
     tell(1)
+    @pl.when(me == root)
+    def _():
+        pl.semaphore_wait(ready, 1)
+        for k in order:
+            hand_over(k, states.at[k]).start()
+
     for k in order:
         load_plane(k).wait()
 
-        @pl.when(away & (lax.rem(me, 2) == k % 2))
+        @pl.when(relay)
         def _(k=k):
-            remote(cur.at[k], cur.at[k], s2.at[k], d1.at[k], mate, dom).start()
+            if k == order[0]:
+                pl.semaphore_wait(ready, 1)
+            hand_over(k, cur.at[k]).start()
 
         perm[4 + k] = jnp.exp(SHRINK * cur[k] + BETA * nz[k])
         here = perm.at[4 + k]
         if k > 0:
-            remote(here, perm.at[k], sn.at[0], dn.at[0], me, slab(1)).start()
+            remote(here, perm.at[k], sn.at[k], dn.at[k], me, slab(1)).start()
         if k < 3:
-            remote(here, perm.at[8 + k], sf.at[0], df.at[0], me, slab(-1)).start()
+            remote(here, perm.at[8 + k], sf.at[k], dn.at[8 + k], me, slab(-1)).start()
     hear(1)
     tell(2)
-    near = [
-        remote(perm.at[pl.ds(5, 3)], perm.at[pl.ds(1, 3)], sn.at[0], dn.at[0], me, slab(1)),
-        remote(perm.at[pl.ds(4, 3)], perm.at[pl.ds(8, 3)], sf.at[0], df.at[0], me, slab(-1)),
-    ]
+    near = {k: remote(perm.at[4 + k], perm.at[k], sn.at[k], dn.at[k], me, slab(1)) for k in (1, 2, 3)}
+    for k in (0, 1, 2):
+        near[8 + k] = remote(perm.at[4 + k], perm.at[8 + k], sf.at[k], dn.at[8 + k], me, slab(-1))
     far = [
-        remote(perm.at[4], perm.at[0], sn.at[1], dn.at[1], me, slab(1)),
-        remote(perm.at[7], perm.at[11], sf.at[1], df.at[1], me, slab(-1)),
+        remote(perm.at[4], perm.at[0], sn.at[0], dn.at[0], me, slab(1)),
+        remote(perm.at[7], perm.at[11], sf.at[3], dn.at[11], me, slab(-1)),
     ]
     for copy in far:
         copy.start()
@@ -362,11 +384,17 @@
         copy.wait_recv()
     finish(5)
     finish(6)
-    for copy in near:
-        copy.wait_recv()
-    for k in (2, 3, 8, 9):
+    for k in (1, 2, 9, 10):
+        near[k].wait_recv()
+    for k in (2, 9):
         sides(k)
-    for k in (1, 2, 3, 7, 8, 9):
+    for k in (1, 9):
+        face(k)
+    for k in (3, 8):
+        near[k].wait_recv()
+    for k in (3, 8):
+        sides(k)
+    for k in (2, 3, 7, 8):
         face(k)
     for k in (2, 3, 4, 7, 8, 9):
         finish(k)
@@ -545,17 +573,15 @@
     @pl.when(me == root)
     def _():
         for k in order:
-            for p in peers:
-                if p // 2 == root // 2 or p % 2 == k % 2:
-                    remote(states.at[k], cur.at[k], s1.at[p, k], d1.at[k], p, dom).wait_send()
-
-    for k in order:
-
-        @pl.when(away & (lax.rem(me, 2) == k % 2))
-        def _(k=k):
-            remote(cur.at[k], cur.at[k], s2.at[k], d1.at[k], mate, dom).wait_send()
-
-    for copies in (sends_src, near, far, sends_q, sends_r):
+            for copy in across(k):
+                copy.wait_send()
+
+    @pl.when(leads)
+    def _():
+        for k in order:
+            hand_over(k, cur.at[k]).wait_send()
+
+    for copies in (sends_src, near.values(), far, sends_q, sends_r):
         for copy in copies:
             copy.wait_send()
     gather_wait(gp2, sp.at[0], dp.at[0]).wait_send()
@@ -585,9 +611,10 @@
         pltpu.VMEM((16, 128), F32),
         pltpu.VMEM((128, 128), F32),
         dma((2,)), dma((props, 4)), dma((4,)), dma((4,)),
-        dma((2,)), dma((2,)), dma((2,)), dma((2,)), dma((2,)), dma((2,)),
+        dma((2,)), dma((2,)), dma((4,)), dma((12,)), dma((4,)),
         dma((6,)), dma((6,)), dma((1,)), dma((1,)), dma((4,)), dma((4,)), dma((1,)), dma((1,)),
         pltpu.SemaphoreType.REGULAR((3, 2)),
+        pltpu.SemaphoreType.REGULAR,
     ]
     hbm = pl.BlockSpec(memory_space=pl.ANY)
 

time: 37.8 us -> 38.5 us (1.019)
  loops' own time: 0.57 us -> 4.18 us
  Pallas kernels: 35.8 us -> 32.9 us
    another operation x1, loops' own time: 0.57 us -> 4.18 us  [body(): return lax.switch(accepted[0], branches, states[0], noise[0], source)[None]]
    pallas_call x1, Pallas kernels: 35.8 us -> 32.9 us  [body(): return lax.switch(accepted[0], branches, states[0], noise[0], source)[None]]
where the time goes in v6:
time: 38.5 us; the launch traced here: 38.4 us
  Pallas kernels  32.9 us (85%)
  loops' own time  4.18 us (11%)
  local copies, waits for them, and re-layouts  0.66 us (2%)
  between operations  0.66 us (2%)
    pallas_call x1, Pallas kernels, body(): return lax.switch(accepted[0], branches, states[0], noise[0], source)[None]  32.9 us
    another operation x1, loops' own time, body(): return lax.switch(accepted[0], branches, states[0], noise[0], source)[None]  4.18 us

profile of v6, /device:TPU:1, one launch (start us, length us, event | category | flops | bytes accessed | tf_op | source)
XLA Modules:
  0.0 38.4 jit_solution(9655380319722497647)
XLA Ops:
  0.7 37.1 %conditional.1 = (f32[1,4,64,128]{3,2,1,0:T(8,128)S(1)}) conditional(s32[]{:T(128)} %bitcast.8, (f32[4,64,128]{2,1,0:T(8,128)}, f32[4,64,128]{2,1,0:T(8,128)}, f32[4,64,128]{2,1,0:T(8,128)}) %tuple.62, (f32[4,64,128]{2,1,0:T(8,128)}, f32[4,64,128]{2,1,0:T(8,128)}, f32[4,64,128]{2,1,0:T(8,128)}) %tuple.63, ...), branch_computations={%region_0.0_spmd, %region_1.0_spmd, %region_2.0_spmd, %region_3.0_... | conditional | bytes 8 | solution.py:633
  4.3 32.9 %mcmc_step_3.1 = f32[4,64,128]{2,1,0:T(8,128)S(1)} custom-call(f32[4,64,128]{2,1,0:T(8,128)} %get-tuple-element.72.states, f32[4,64,128]{2,1,0:T(8,128)} %get-tuple-element.73.noise, f32[4,64,128]{2,1,0:T(8,128)} %get-tuple-element.74.source), custom_call_target="tpu_custom_call" | custom-call | tf_op jit(solution)/shard_map/cond/branch_3_fun/mcmc_step_3/pallas_call | solution.py:633
  37.8 0.7 %copy.22 = f32[1,4,64,128]{3,2,1,0:T(8,128)} copy(f32[1,4,64,128]{3,2,1,0:T(8,128)S(1)} %get-tuple-element.87) | data formatting | bytes 262144

commit v7 on v6

--- a/solution.py
+++ b/solution.py
@@ -26,14 +26,12 @@
     return jnp.where(mask, 1.0, 0.0).astype(BF16)
 
 
-def dot3(x, matrix):
+def dot2(x, matrix):
     rows = x.shape[0]
     hi = x.astype(BF16).astype(F32)
-    rest = x - hi
-    mid = rest.astype(BF16).astype(F32)
-    stacked = jnp.concatenate([hi, mid, rest - mid], axis=0).astype(BF16)
+    stacked = jnp.concatenate([hi, x - hi], axis=0).astype(BF16)
     y = jnp.dot(stacked, matrix, preferred_element_type=F32)
-    return y[:rows] + y[rows : 2 * rows] + y[2 * rows :]
+    return y[:rows] + y[rows:]
 
 
 def up(v, axis, by=1):
@@ -180,6 +178,31 @@
             device_id=(p, d), device_id_type=MESH,
         )
 
+    def within(o):
+        return (dom + o >= 0) & (dom + o < doms)
+
+    class Along:
+        def __init__(self, from_ref, to_ref, send, recv, o):
+            self.copy = remote(from_ref, to_ref, send, recv, me, slab(o))
+            self.to, self.source = within(o), within(-o)
+
+        def start(self):
+            pl.when(self.to)(self.copy.start)
+
+        def wait_send(self):
+            pl.when(self.to)(self.copy.wait_send)
+
+        def wait_recv(self):
+            pl.when(self.source)(self.copy.wait_recv)
+
+    @pl.when((dom < 3) | (dom >= doms - 3))
+    def _():
+        for first in (0, 8):
+            perm[pl.ds(first, 4)] = jnp.ones((4, 64, 128), F32)
+            src[pl.ds(first, 4)] = jnp.zeros((4, 64, 128), F32)
+        perm1[...] = jnp.ones(perm1.shape, F32)
+        right1[...] = jnp.zeros(right1.shape, F32)
+
     load_noise = pltpu.make_async_copy(noise, nz, loc.at[0])
     load_source = pltpu.make_async_copy(source, src.at[pl.ds(4, 4)], loc.at[1])
     load_noise.start()
@@ -204,10 +227,15 @@
     def _():
         pl.semaphore_signal(barrier, inc=1, device_id=(mate, dom), device_id_type=MESH)
 
-    for o in (1, -1, 2, -2, 3, -3):
-        pl.semaphore_signal(barrier, inc=1, device_id=(me, slab(o)), device_id_type=MESH)
+    for o in (1, -1, 2, -2, 3, -3, 4, -4):
+
+        @pl.when(within(o))
+        def _(o=o):
+            pl.semaphore_signal(barrier, inc=1, device_id=(me, slab(o)), device_id_type=MESH)
+
+    beside = jnp.minimum(dom, 4) + jnp.minimum(doms - 1 - dom, 4)
     extra = jnp.where(me == root, props // 2 - 1, jnp.where(leads, 0, 1))
-    pl.semaphore_wait(barrier, 6 + extra)
+    pl.semaphore_wait(barrier, beside + extra)
 
     @pl.when(jnp.logical_not(leads))
     def _():
@@ -230,22 +258,28 @@
                 copy.start()
             load_plane(k).start()
 
-    reach = (3, 6, 12)
+    reach = (4, 8, 16)
 
     def tell(i):
         for side, o in enumerate((reach[i], -reach[i])):
-            target = (me, slab(o))
-            pl.semaphore_signal(word.at[i, side], inc=1, device_id=target, device_id_type=MESH)
+
+            @pl.when(within(o))
+            def _(side=side, o=o):
+                target = (me, slab(o))
+                pl.semaphore_signal(word.at[i, side], inc=1, device_id=target, device_id_type=MESH)
 
     def hear(i):
-        for side in range(2):
-            pl.semaphore_wait(word.at[i, side], 1)
+        for side, o in enumerate((reach[i], -reach[i])):
+
+            @pl.when(within(-o))
+            def _(side=side):
+                pl.semaphore_wait(word.at[i, side], 1)
 
     tell(0)
 
     sends_src = [
-        remote(source.at[pl.ds(1, 3)], src.at[pl.ds(1, 3)], ss.at[0], ds_.at[0], me, slab(1)),
-        remote(source.at[pl.ds(0, 3)], src.at[pl.ds(8, 3)], ss.at[1], ds_.at[1], me, slab(-1)),
+        Along(source.at[pl.ds(1, 3)], src.at[pl.ds(1, 3)], ss.at[0], ds_.at[0], 1),
+        Along(source.at[pl.ds(0, 3)], src.at[pl.ds(8, 3)], ss.at[1], ds_.at[1], -1),
     ]
     for copy in sends_src:
         copy.start()
@@ -268,13 +302,15 @@
     edges = edges + jnp.where(lane == 0, 1.0, 0.0) + jnp.where(lane == 127, 1.0, 0.0)
 
     load_noise.wait()
-    hear(0)
-    tell(1)
     @pl.when(me == root)
     def _():
         pl.semaphore_wait(ready, 1)
         for k in order:
             hand_over(k, states.at[k]).start()
+
+    near = {k: Along(perm.at[4 + k], perm.at[k], sn.at[k], dn.at[k], 1) for k in (1, 2, 3)}
+    for k in (0, 1, 2):
+        near[8 + k] = Along(perm.at[4 + k], perm.at[8 + k], sf.at[k], dn.at[8 + k], -1)
 
     for k in order:
         load_plane(k).wait()
@@ -286,19 +322,15 @@
             hand_over(k, cur.at[k]).start()
 
         perm[4 + k] = jnp.exp(SHRINK * cur[k] + BETA * nz[k])
-        here = perm.at[4 + k]
         if k > 0:
-            remote(here, perm.at[k], sn.at[k], dn.at[k], me, slab(1)).start()
+            near[k].start()
         if k < 3:
-            remote(here, perm.at[8 + k], sf.at[k], dn.at[8 + k], me, slab(-1)).start()
-    hear(1)
-    tell(2)
-    near = {k: remote(perm.at[4 + k], perm.at[k], sn.at[k], dn.at[k], me, slab(1)) for k in (1, 2, 3)}
-    for k in (0, 1, 2):
-        near[8 + k] = remote(perm.at[4 + k], perm.at[8 + k], sf.at[k], dn.at[8 + k], me, slab(-1))
+            near[8 + k].start()
+    hear(0)
+    tell(1)
     far = [
-        remote(perm.at[4], perm.at[0], sn.at[0], dn.at[0], me, slab(1)),
-        remote(perm.at[7], perm.at[11], sf.at[3], dn.at[11], me, slab(-1)),
+        Along(perm.at[4], perm.at[0], sn.at[0], dn.at[0], 1),
+        Along(perm.at[7], perm.at[11], sf.at[3], dn.at[11], -1),
     ]
     for copy in far:
         copy.start()
@@ -308,7 +340,7 @@
         for i in range(2):
             tmp[...] = planes[2 * i] + planes[2 * i + 1]
             sums.append(pair_rows(tmp, 32))
-        return dot3(jnp.concatenate(sums, axis=1), c01)
+        return dot2(jnp.concatenate(sums, axis=1), c01)
 
     def restrict12(value):
         tmp2[...] = value
@@ -316,15 +348,17 @@
         for q in range(4):
             low = tmp2[pl.ds(2 * q, 4, stride=8), :]
             parts.append(low + tmp2[pl.ds(2 * q + 1, 4, stride=8), :])
-        return dot3(jnp.concatenate(parts, axis=1), c12)
+        return dot2(jnp.concatenate(parts, axis=1), c12)
 
     own1 = 0.125 * restrict01([perm[k] for k in range(4, 8)])
     perm1[3] = own1
     sends_q = []
     for i, o in enumerate((1, -1, 2, -2, 3, -3)):
-        copy = remote(perm1.at[3], perm1.at[3 - o], sq.at[i], dq.at[i], me, slab(o))
+        copy = Along(perm1.at[3], perm1.at[3 - o], sq.at[i], dq.at[i], o)
         copy.start()
         sends_q.append(copy)
+    hear(1)
+    tell(2)
     gp2[dom] = 0.125 * restrict12(own1)
 
     def gather_to(buf, send, recv):
@@ -339,8 +373,6 @@
         part = buf.at[pl.ds(0, doms - 1)]
         return remote(part, part, send, recv, me, slab(1))
 
-    hear(2)
-    gather_to(gp2, sp.at[0], dp.at[0])
 
     def sides(k):
         p = perm[k]
@@ -407,9 +439,11 @@
     right1[2] = restrict01(rest)
     sends_r = []
     for i, o in enumerate((1, -1, 2, -2)):
-        copy = remote(right1.at[2], right1.at[2 - o], sr.at[i], dr.at[i], me, slab(o))
+        copy = Along(right1.at[2], right1.at[2 - o], sr.at[i], dr.at[i], o)
         copy.start()
         sends_r.append(copy)
+    hear(2)
+    gather_to(gp2, sp.at[0], dp.at[0])
 
     for copy in sends_q:
         copy.wait_recv()
@@ -457,7 +491,7 @@
         for g in range(8):
             low, high = both[16 * g : 16 * g + 8], moved[16 * g + 8 : 16 * g + 16]
             parts.append(jnp.where(row8 < 4, low, high))
-        y = dot3(jnp.concatenate(parts, axis=0), c23)
+        y = dot2(jnp.concatenate(parts, axis=0), c23)
         total = tree_sum([jnp.where(group[g], y[8 * g : 8 * g + 8], 0.0) for g in range(8)])
         for parity in range(2):
             for q in range(2):
@@ -473,7 +507,7 @@
             rows = [tmp3[pl.ds(8 * parity + q, 4, stride=2), :] for parity in range(2)]
             halves.append(jnp.concatenate(rows, axis=0))
         e = jnp.concatenate(halves, axis=1)
-        y = dot3(jnp.concatenate([jnp.where(m, e, 0.0) for m in group], axis=0), c32)
+        y = dot2(jnp.concatenate([jnp.where(m, e, 0.0) for m in group], axis=0), c32)
         parts = []
         for g in range(8):
             value = y[8 * g : 8 * g + 8]
@@ -547,7 +581,7 @@
         z = slab(j)
         value = e2s[pl.ds(pl.multiple_of((z // 2) * 8, 8), 8), :]
         parts.append(jnp.where(lax.rem(z, 2) == 0, value, pltpu.roll(value, 4, 0)))
-    wide1 = dot3(jnp.concatenate(parts, axis=0), c21)
+    wide1 = dot2(jnp.concatenate(parts, axis=0), c21)
     for j in range(5):
         for q in range(4):
             piece = wide1[8 * j : 8 * j + 4, 128 * q : 128 * q + 128]
@@ -559,7 +593,7 @@
     for _ in range(2):
         v1 = sweep(v1, b1, all1, MOVES1)
 
-    fine = dot3(v1[32:128], c10)
+    fine = dot2(v1[32:128], c10)
     for k, i, half in ((2, 0, 1), (4, 1, 0), (6, 1, 1), (8, 2, 0)):
         repeat_rows(tmp, fine[32 * i : 32 * i + 32, 128 * half : 128 * half + 128])
         add = tmp[...]

time: 38.5 us -> 37.8 us (0.982)
  loops' own time: 4.18 us -> 0.9 us
  Pallas kernels: 32.9 us -> 35.4 us
    another operation x1, loops' own time: 4.18 us -> 0.9 us  [body(): return lax.switch(accepted[0], branches, states[0], noise[0], source)[None]]
    pallas_call x1, Pallas kernels: 32.9 us -> 35.4 us  [body(): return lax.switch(accepted[0], branches, states[0], noise[0], source)[None]]
where the time goes in v7:
time: 37.8 us; the launch traced here: 37.6 us
  Pallas kernels  35.4 us (94%)
  loops' own time  0.9 us (2%)
  local copies, waits for them, and re-layouts  0.66 us (2%)
  between operations  0.66 us (2%)
    pallas_call x1, Pallas kernels, body(): return lax.switch(accepted[0], branches, states[0], noise[0], source)[None]  35.4 us
    another operation x1, loops' own time, body(): return lax.switch(accepted[0], branches, states[0], noise[0], source)[None]  0.9 us

profile of v7, /device:TPU:1, one launch (start us, length us, event | category | flops | bytes accessed | tf_op | source)
XLA Modules:
  0.0 37.6 jit_solution(10854569471611895277)
XLA Ops:
  0.7 36.3 %conditional.1 = (f32[1,4,64,128]{3,2,1,0:T(8,128)S(1)}) conditional(s32[]{:T(128)} %bitcast.8, (f32[4,64,128]{2,1,0:T(8,128)}, f32[4,64,128]{2,1,0:T(8,128)}, f32[4,64,128]{2,1,0:T(8,128)}) %tuple.62, (f32[4,64,128]{2,1,0:T(8,128)}, f32[4,64,128]{2,1,0:T(8,128)}, f32[4,64,128]{2,1,0:T(8,128)}) %tuple.63, ...), branch_computations={%region_0.0_spmd, %region_1.0_spmd, %region_2.0_spmd, %region_3.0_... | conditional | bytes 8 | solution.py:667
  0.9 35.4 %mcmc_step_6.1 = f32[4,64,128]{2,1,0:T(8,128)S(1)} custom-call(f32[4,64,128]{2,1,0:T(8,128)} %get-tuple-element.81.states, f32[4,64,128]{2,1,0:T(8,128)} %get-tuple-element.82.noise, f32[4,64,128]{2,1,0:T(8,128)} %get-tuple-element.83.source), custom_call_target="tpu_custom_call" | custom-call | tf_op jit(solution)/shard_map/cond/branch_6_fun/mcmc_step_6/pallas_call | solution.py:667
  37.0 0.7 %copy.22 = f32[1,4,64,128]{3,2,1,0:T(8,128)} copy(f32[1,4,64,128]{3,2,1,0:T(8,128)S(1)} %get-tuple-element.87) | data formatting | bytes 262144
